TPU v7x, 32 devices: a whole 2x2x4 slice. The times are simulated.
32 devices in a mesh: dp: 8 (over y, x, core), mp: 4 (over z).
Axes of the slice: x: 2, y: 2, z: 4, core: 2. Of those that a mesh axis runs over, the one named last changes fastest.
Arguments:
- tokens: bfloat16 [16, 1024, 768], P('dp', 'mp'), may hold values from -6 to 6
- segment_ids: int32 [16, 1024], P('dp'), may hold values from 0 to 3, never falling along the last dimension, each value on 1 to 512 neighbouring positions
- mask_flags: int32 [16, 1024], P('dp', 'mp'), may hold values 0 or 1
- mask_embed: float32 [768], replicated, may hold values from -4 to 4
- first_gain: float32 [768], replicated, may hold values from 0.5 to 1.5
- first_shift: float32 [768], replicated, may hold values from -1.2 to 1.2
- query_key_value_weight: bfloat16 [3, 768, 768], P(None, None, 'mp'), may hold values from -0.21875 to 0.21875
- qv_bias: float32 [2, 768], P(None, 'mp'), may hold values from -2 to 2
- output_weight: bfloat16 [768, 768], P('mp'), may hold values from -1.75 to 1.75
- out_bias: float32 [768], replicated, may hold values from -1.2 to 1.2
- second_gain: float32 [768], replicated, may hold values from 0.5 to 1.5
- second_shift: float32 [768], replicated, may hold values from -1.2 to 1.2
- up_weight: bfloat16 [768, 3072], P(None, 'mp'), may hold values from -0.21875 to 0.21875
- expand_bias: float32 [3072], P('mp'), may hold values from -2 to 2
- down_weight: bfloat16 [3072, 768], P('mp'), may hold values from -0.109375 to 0.109375
- down_bias: float32 [768], replicated, may hold values from -1.2 to 1.2
- out_grad: bfloat16 [16, 1024, 768], P('dp', 'mp'), may hold values from -6 to 6
Outputs:
- activations: bfloat16 [16, 1024, 768], P('dp', 'mp')
- tokens_grad: float32 [16, 1024, 768], P('dp', 'mp')
- mask_embed_grad: float32 [768], replicated
- first_gain_grad: float32 [768], replicated
- first_shift_grad: float32 [768], replicated
- w_qkv_grad: float32 [3, 768, 768], P(None, None, 'mp')
- qv_bias_grad: float32 [2, 768], P(None, 'mp')
- w_out_grad: float32 [768, 768], P('mp')
- out_bias_grad: float32 [768], replicated
- second_gain_grad: float32 [768], replicated
- second_shift_grad: float32 [768], replicated
- up_weight_grad: float32 [768, 3072], P(None, 'mp')
- up_bias_grad: float32 [3072], P('mp')
- down_weight_grad: float32 [3072, 768], P('mp')
- down_bias_grad: float32 [768], replicated
Inputs may be any that keep to these rules, and one draw needn't show every extreme that they name: `segment_ids`: in each row the ids never fall; each segment holds 1 to 512 positions, and one holds exactly 512.
All inputs are finite; a program needn't handle non-finite values. No bound on the sum of `mask_flags` on one device may be relied on, other than what follows from the above.
Results may differ from a plain program's by a relative error of at most 0.015.
Values may be sent and summed in bfloat16 or wider, within the bound.
No kernel may reach another device: no remote copies, remote signals or barrier semaphores. Data moves between devices by JAX's collectives and lax.ppermute only.
A program may use at most 128 MiB of HBM per device.

v0:
```python
import jax
import jax.numpy as jnp
from jax import lax
from jax.sharding import PartitionSpec as P

HD = 64


EPSILON = 1e-06
NEG_FILL = -1e30


def normalize(rows, gain, shift):
    row_mean = jnp.mean(rows, axis=-1, keepdims=True)
    centred = rows - row_mean
    variance = jnp.mean(centred * centred, axis=-1, keepdims=True)
    inv_scale = lax.rsqrt(variance + EPSILON)
    unit_rows = centred * inv_scale
    return (unit_rows * gain + shift, unit_rows, inv_scale)


def normalize_back(incoming, unit_rows, inv_scale, gain):
    scaled = incoming * gain
    inner_one = jnp.mean(scaled, axis=-1, keepdims=True)
    inner_two = jnp.mean(scaled * unit_rows, axis=-1, keepdims=True)
    grad_rows = inv_scale * (scaled - inner_one - unit_rows * inner_two)
    return (grad_rows, jnp.sum(incoming * unit_rows, axis=(0, 1)), jnp.sum(incoming, axis=(0, 1)))


def gelu_exact(values):
    return jax.nn.gelu(values, approximate=False)


def score_block(query_blk, seg_query, key_rows, seg_row):
    scores = jnp.einsum(
        "qhd,khd->hqk", query_blk, key_rows, preferred_element_type=jnp.float32
    ) * HD ** (-0.5)
    same_seg = seg_query[:, None] == seg_row[None, :]
    return jnp.where(same_seg[None, :, :], scores, NEG_FILL)


def attend_sequence(seq_items):
    queries, key_rows, value_rows, seg_row = seq_items
    length = queries.shape[0]
    block_rows = min(512, length)
    block_count = length // block_rows

    def one_block(block_items):
        query_blk, seg_query = block_items
        scores = score_block(query_blk, seg_query, key_rows, seg_row)
        row_max = jnp.max(scores, axis=-1, keepdims=True)
        exp_scores = jnp.exp(scores - row_max)
        row_total = jnp.sum(exp_scores, axis=-1, keepdims=True)
        attn_probs = (exp_scores / row_total).astype(jnp.bfloat16)
        context_rows = jnp.einsum(
            "hqk,khd->qhd", attn_probs, value_rows, preferred_element_type=jnp.float32
        )
        return (context_rows.astype(jnp.bfloat16), (row_max + jnp.log(row_total))[:, :, 0])

    query_blocks = queries.reshape((block_count, block_rows) + queries.shape[1:])
    seg_blocks = seg_row.reshape(block_count, block_rows)
    contexts, log_total = lax.map(one_block, (query_blocks, seg_blocks))
    return (contexts.reshape(length, -1), log_total)


def attend_back(seq_items):
    queries, key_rows, value_rows, seg_row, log_total, grad_context = seq_items
    length = queries.shape[0]
    block_rows = min(512, length)
    block_count = length // block_rows
    score_scale = HD ** (-0.5)

    def one_block(running, block_items):
        query_blk, seg_query, total_blk, grad_blk = block_items
        scores = score_block(query_blk, seg_query, key_rows, seg_row)
        attn_probs = jnp.exp(scores - total_blk[:, :, None])
        grad_probs = jnp.einsum(
            "qhd,khd->hqk", grad_blk, value_rows, preferred_element_type=jnp.float32
        )
        row_dot = jnp.sum(attn_probs * grad_probs, axis=-1, keepdims=True)
        grad_scores = (attn_probs * (grad_probs - row_dot)).astype(jnp.bfloat16)
        grad_query = (
            jnp.einsum("hqk,khd->qhd", grad_scores, key_rows, preferred_element_type=jnp.float32)
            * score_scale
        )
        grad_keys = (
            running[0]
            + jnp.einsum("hqk,qhd->khd", grad_scores, query_blk, preferred_element_type=jnp.float32)
            * score_scale
        )
        grad_values = running[1] + jnp.einsum(
            "hqk,qhd->khd",
            attn_probs.astype(jnp.bfloat16),
            grad_blk,
            preferred_element_type=jnp.float32,
        )
        return ((grad_keys, grad_values), grad_query.astype(jnp.bfloat16))

    zero_rows = jnp.zeros(key_rows.shape, jnp.float32)
    query_blocks = queries.reshape((block_count, block_rows) + queries.shape[1:])
    grad_blocks = grad_context.reshape((block_count, block_rows) + grad_context.shape[1:])
    seg_blocks = seg_row.reshape(block_count, block_rows)
    (grad_keys, grad_values), grad_queries = lax.scan(
        one_block, (zero_rows, zero_rows), (query_blocks, seg_blocks, log_total, grad_blocks)
    )
    return (
        grad_queries.reshape(length, -1),
        grad_keys.astype(jnp.bfloat16).reshape(length, -1),
        grad_values.astype(jnp.bfloat16).reshape(length, -1),
    )


def forward_pass(
    tokens,
    segment_ids,
    masked,
    mask_embed,
    first_gain,
    first_shift,
    query_key_value_weight,
    qv_bias,
    output_weight,
    out_bias,
    second_gain,
    second_shift,
    up_weight,
    expand_bias,
    down_weight,
    down_bias,
):
    start_rows = jnp.where(masked, mask_embed, tokens.astype(jnp.float32))
    first_normalized, unit_one, inv_one = normalize(start_rows, first_gain, first_shift)
    complete_first = lax.all_gather(first_normalized.astype(jnp.bfloat16), "mp", axis=1, tiled=True)
    projected_rows = jnp.einsum(
        "gaw,pwn->pgan", complete_first, query_key_value_weight, preferred_element_type=jnp.float32
    )
    seq_count = complete_first.shape[0]
    length = complete_first.shape[1]
    heads_here = query_key_value_weight.shape[2] // HD

    def to_heads(projection):
        return projection.astype(jnp.bfloat16).reshape(seq_count, length, heads_here, HD)

    queries = to_heads(projected_rows[0] + qv_bias[0])
    key_rows = to_heads(projected_rows[1])
    value_rows = to_heads(projected_rows[2] + qv_bias[1])
    context_rows, log_total = lax.map(attend_sequence, (queries, key_rows, value_rows, segment_ids))
    attention_partial = jnp.einsum(
        "itq,qp->itp", context_rows, output_weight, preferred_element_type=jnp.float32
    )
    attention_total = lax.psum_scatter(attention_partial, "mp", scatter_dimension=1, tiled=True)
    mid_rows = start_rows + attention_total + out_bias
    second_normalized, unit_two, inv_two = normalize(mid_rows, second_gain, second_shift)
    complete_second = lax.all_gather(
        second_normalized.astype(jnp.bfloat16), "mp", axis=1, tiled=True
    )
    hidden_rows = (
        jnp.einsum("coz,zb->cob", complete_second, up_weight, preferred_element_type=jnp.float32)
        + expand_bias
    )
    active_tokens = gelu_exact(hidden_rows).astype(jnp.bfloat16)
    feedforward_partial = jnp.einsum(
        "oci,iz->ocz", active_tokens, down_weight, preferred_element_type=jnp.float32
    )
    feedforward_total = lax.psum_scatter(
        feedforward_partial.astype(jnp.bfloat16), "mp", scatter_dimension=1, tiled=True
    ).astype(jnp.float32)
    final_rows = mid_rows + feedforward_total + down_bias
    return (
        final_rows,
        unit_one,
        inv_one,
        complete_first,
        queries,
        key_rows,
        value_rows,
        log_total,
        context_rows,
        unit_two,
        inv_two,
        complete_second,
        hidden_rows,
        active_tokens,
    )


def body(
    tokens,
    segment_ids,
    mask_flags,
    mask_embed,
    first_gain,
    first_shift,
    query_key_value_weight,
    qv_bias,
    output_weight,
    out_bias,
    second_gain,
    second_shift,
    up_weight,
    expand_bias,
    down_weight,
    down_bias,
    out_grad,
):
    masked = (mask_flags == 1)[:, :, None]
    operands = (
        tokens,
        segment_ids,
        masked,
        mask_embed,
        first_gain,
        first_shift,
        query_key_value_weight,
        qv_bias,
        output_weight,
        out_bias,
        second_gain,
        second_shift,
        up_weight,
        expand_bias,
        down_weight,
        down_bias,
    )
    saved = forward_pass(*operands)
    final_rows = saved[0]
    (
        unit_one,
        inv_one,
        complete_first,
        queries,
        key_rows,
        value_rows,
        log_total,
        context_rows,
        unit_two,
        inv_two,
        complete_second,
        hidden_rows,
        active_tokens,
    ) = saved[1:]
    grad_out = out_grad.astype(jnp.float32)
    complete_grad = lax.all_gather(out_grad, "mp", axis=1, tiled=True)
    down_weight_grad = jnp.einsum(
        "bcj,bca->ja", active_tokens, complete_grad, preferred_element_type=jnp.float32
    )
    down_bias_grad = jnp.sum(grad_out, axis=(0, 1))
    active_gradient = jnp.einsum(
        "xku,qu->xkq", complete_grad, down_weight, preferred_element_type=jnp.float32
    )
    gelu_pull = jax.vjp(gelu_exact, hidden_rows)[1]
    hidden_gradient = gelu_pull(active_gradient)[0].astype(jnp.bfloat16)
    up_bias_grad = jnp.sum(hidden_gradient, axis=(0, 1), dtype=jnp.float32)
    up_weight_grad = jnp.einsum(
        "han,hav->nv", complete_second, hidden_gradient, preferred_element_type=jnp.float32
    )
    second_partial = jnp.einsum(
        "qtp,kp->qtk", hidden_gradient, up_weight, preferred_element_type=jnp.float32
    )
    grad_normed_two = lax.psum_scatter(
        second_partial.astype(jnp.bfloat16), "mp", scatter_dimension=1, tiled=True
    ).astype(jnp.float32)
    grad_mid, second_gain_grad, second_shift_grad = normalize_back(
        grad_normed_two, unit_two, inv_two, second_gain
    )
    grad_mid = grad_mid + grad_out
    out_bias_grad = jnp.sum(grad_mid, axis=(0, 1))
    complete_attention_grad = lax.all_gather(
        grad_mid.astype(jnp.bfloat16), "mp", axis=1, tiled=True
    )
    w_out_grad = jnp.einsum(
        "kgz,kgj->zj", context_rows, complete_attention_grad, preferred_element_type=jnp.float32
    )
    grad_context = jnp.einsum(
        "zwm,km->zwk", complete_attention_grad, output_weight, preferred_element_type=jnp.float32
    ).astype(jnp.bfloat16)
    grad_heads = grad_context.reshape(queries.shape)
    grad_q_rows, grad_k_rows, grad_v_rows = lax.map(
        attend_back, (queries, key_rows, value_rows, segment_ids, log_total, grad_heads)
    )
    gradient_stack = jnp.stack([grad_q_rows, grad_k_rows, grad_v_rows])
    w_qkv_grad = jnp.einsum(
        "bpz,tbpv->tzv", complete_first, gradient_stack, preferred_element_type=jnp.float32
    )
    qv_bias_grad = jnp.stack(
        [
            jnp.sum(grad_q_rows, axis=(0, 1), dtype=jnp.float32),
            jnp.sum(grad_v_rows, axis=(0, 1), dtype=jnp.float32),
        ]
    )
    first_partial = jnp.einsum(
        "rvfy,rwy->vfw", gradient_stack, query_key_value_weight, preferred_element_type=jnp.float32
    )
    grad_normed_one = lax.psum_scatter(
        first_partial.astype(jnp.bfloat16), "mp", scatter_dimension=1, tiled=True
    ).astype(jnp.float32)
    grad_start, first_gain_grad, first_shift_grad = normalize_back(
        grad_normed_one, unit_one, inv_one, first_gain
    )
    grad_start = grad_start + grad_mid
    mask_embed_grad = jnp.sum(jnp.where(masked, grad_start, 0.0), axis=(0, 1))
    tokens_grad = jnp.where(masked, 0.0, grad_start)
    (
        mask_embed_grad,
        first_gain_grad,
        first_shift_grad,
        out_bias_grad,
        second_gain_grad,
        second_shift_grad,
        down_bias_grad,
    ) = lax.psum(
        (
            mask_embed_grad,
            first_gain_grad,
            first_shift_grad,
            out_bias_grad,
            second_gain_grad,
            second_shift_grad,
            down_bias_grad,
        ),
        "mp",
    )
    (
        w_qkv_grad,
        qv_bias_grad,
        w_out_grad,
        up_weight_grad,
        up_bias_grad,
        down_weight_grad,
        mask_embed_grad,
        first_gain_grad,
        first_shift_grad,
        out_bias_grad,
        second_gain_grad,
        second_shift_grad,
        down_bias_grad,
    ) = lax.psum(
        (
            w_qkv_grad,
            qv_bias_grad,
            w_out_grad,
            up_weight_grad,
            up_bias_grad,
            down_weight_grad,
            mask_embed_grad,
            first_gain_grad,
            first_shift_grad,
            out_bias_grad,
            second_gain_grad,
            second_shift_grad,
            down_bias_grad,
        ),
        "dp",
    )
    return (
        final_rows.astype(jnp.bfloat16),
        tokens_grad,
        mask_embed_grad,
        first_gain_grad,
        first_shift_grad,
        w_qkv_grad,
        qv_bias_grad,
        w_out_grad,
        out_bias_grad,
        second_gain_grad,
        second_shift_grad,
        up_weight_grad,
        up_bias_grad,
        down_weight_grad,
        down_bias_grad,
    )


def solution(mesh):
    in_specs = (
        P("dp", "mp", None),
        P("dp", None),
        P("dp", "mp"),
        P(),
        P(),
        P(),
        P(None, None, "mp"),
        P(None, "mp"),
        P("mp", None),
        P(),
        P(),
        P(),
        P(None, "mp"),
        P("mp"),
        P("mp", None),
        P(),
        P("dp", "mp", None),
    )
    out_specs = (
        P("dp", "mp", None),
        P("dp", "mp", None),
        P(),
        P(),
        P(),
        P(None, None, "mp"),
        P(None, "mp"),
        P("mp", None),
        P(),
        P(),
        P(),
        P(None, "mp"),
        P("mp"),
        P("mp", None),
        P(),
    )
    return jax.shard_map(body, mesh=mesh, in_specs=in_specs, out_specs=out_specs, check_vma=False)
```

profile of v0, /device:TPU:0, one launch (start us, length us, event | category | flops | bytes accessed | tf_op | source)
XLA Modules:
  0.0 855.7 jit_solution(7781445110868219297)
XLA Ops:
  9.5 1.6 multiply_reduce_fusion.2
  11.1 2.5 add_convert_fusion.5
  13.8 66.1 %all-gather.5.cloned.1.call-done = bf16[2,1024,768]{2,1,0:T(8,128)(2,1)} async-done(((bf16[2,256,768]{2,1,0:T(8,128)(2,1)}), bf16[2,1024,768]{2,1,0:T(8,128)(2,1)}) %all-gather.5.cloned.1.call-update) | async-done | bytes 3145744 | tf_op jit(solution)/shard_map/all_gather | solution.py:133
  79.9 4.1 fusion.53
  86.6 44.0 %while.54 = (s32[]{:T(128)}, bf16[2,1024,192]{1,2,0:T(8,128)(2,1)}, f32[2,2,3,512]{3,2,1,0:T(4,128)}, bf16[2,1024,3,64]{1,3,2,0:T(8,128)(2,1)}, s32[2,1024]{1,0:...) while((s32[]{:T(128)}, bf16[2,1024,192]{1,2,0:T(8,128)(2,1)}, ...), condition=%wide.region_7.8_spmd, body=%wide.region_2.7_spmd.sunk | while | flops 422148608 | bytes 33382876 | solution.py:147
  90.7 14.2 %while.57 = (s32[]{:T(128)}, bf16[2,512,3,64]{1,3,2,0:T(8,128)(2,1)}, f32[2,3,512]{2,1,0:T(4,128)}, s32[2,512]{1,0:T(2,128)S(1)}, s32[1024]{0:T(1024)S(1)}, /*in...) while((s32[]{:T(128)}, ...), condition=%wide.region_6.6_spmd, body=%wide.region_3.5_spmd.sunk | while | flops 422148608 | bytes 27037952 | solution.py:62
  92.5 1.8 fusion.154
  94.3 2.1 fusion.155
  99.5 1.8 fusion.154
  101.3 2.1 fusion.155
  112.7 14.2 %while.57 = (s32[]{:T(128)}, bf16[2,512,3,64]{1,3,2,0:T(8,128)(2,1)}, f32[2,3,512]{2,1,0:T(4,128)}, s32[2,512]{1,0:T(2,128)S(1)}, s32[1024]{0:T(1024)S(1)}, /*in...) while((s32[]{:T(128)}, ...), condition=%wide.region_6.6_spmd, body=%wide.region_3.5_spmd.sunk | while | flops 422148608 | bytes 27037952 | solution.py:62
  114.5 1.8 fusion.154
  116.3 2.1 fusion.155
  121.6 1.8 fusion.154
  123.3 2.1 fusion.155
  130.6 5.2 fusion.87
  135.9 109.5 %reduce-scatter.5.cloned.1.call-done = f32[2,256,768]{2,1,0:T(8,128)} async-done(((f32[2,1024,768]{2,1,0:T(8,128)}), f32[2,256,768]{2,1,0:T(8,128)}) %reduce-scatter.5.cloned.1.call-update) | async-done | bytes 1572880 | tf_op jit(solution)/shard_map/reduce_scatter | solution.py:151
  245.5 2.1 fusion.95
  249.7 11.9 %reduce-scatter.9.cloned.1.call-start = ((), (), s32[]{:S(2)}) async-start(), calls=%async_computation.9 | async-start | bytes 3932160 | tf_op jit(solution)/shard_map/reduce_scatter | solution.py:260
  261.6 51.6 %all-gather.7.cloned.1.call-done = bf16[2,1024,768]{2,1,0:T(8,128)(2,1)} async-done(((bf16[2,256,768]{2,1,0:T(8,128)(2,1)}), bf16[2,1024,768]{2,1,0:T(8,128)(2,1)}) %all-gather.7.cloned.1.call-update) | async-done | bytes 3145744 | tf_op jit(solution)/shard_map/all_gather | solution.py:154
  313.2 6.4 fusion.75
  319.6 2.7 copy-done.16
  322.3 15.7 %multiply_convert_fusion.1 = (bf16[2,1024,768]{2,1,0:T(8,128)(2,1)}, f32[2,1024,768]{2,1,0:T(8,128)}) fusion(f32[2,1024,768]{2,1,0:T(8,128)S(1)} %get-tuple-element.410, f32[768]{0:T(1024)S(1)} %copy-done.46, u8[1024,768]{1,0:T(8,128)(4,1)S(1)} %get-tuple-element.280, u8[1024,768]{1,0:T(8,128)(4,1)S(1)} %get-tuple-element.279), kind=kLoop, calls=%fused_computation.77 | loop fusion | flops 111673344 | bytes 17304576 | tf_op jit(solution)/shard_map/convert_element_type | solution.py:161
  338.1 38.8 %all-gather.9.cloned.1.call-done = bf16[2,1024,768]{2,1,0:T(8,128)(2,1)} async-done(((bf16[2,256,768]{2,1,0:T(8,128)(2,1)}), bf16[2,1024,768]{2,1,0:T(8,128)(2,1)}) %all-gather.9.cloned.1.call-update) | async-done | bytes 3145744 | tf_op jit(solution)/shard_map/all_gather | solution.py:243
  376.8 11.1 %convert_reduce_fusion = (f32[768]{0:T(1024)}, bf16[2,1024,768]{2,1,0:T(8,128)(2,1)S(1)}) fusion(f32[2,1024,768]{2,1,0:T(8,128)} %get-tuple-element.392, bf16[2,1024,768]{2,1,0:T(8,128)(2,1)} %all-gather.9.cloned.1.call-done, bf16[768,768]{1,0:T(8,128)(2,1)} %param.39, f32[2,1024,768]{2,1,0:T(8,128)} %copy-done.16, f32[768]{0:T(1024)S(1)} %copy-done.46), kind=kOutput, calls=%fused_computation.75 | convolution fusion | flops 2442657024 | bytes 20060160 | tf_op jit(solution)/shard_map/xku,qu->xkq/dot_general | solution.py:248
  387.9 1.6 copy-done.53
  389.6 4.0 convolution_convert_fusion
  394.8 6.2 convolution_convert_fusion.1
  401.1 51.6 %reduce-scatter.9.cloned.1.call-done = bf16[2,256,768]{2,1,0:T(8,128)(2,1)} async-done(((bf16[2,1024,768]{2,1,0:T(8,128)(2,1)}), bf16[2,256,768]{2,1,0:T(8,128)(2,1)}) %reduce-scatter.9.cloned.1.call-update) | async-done | bytes 786448 | tf_op jit(solution)/shard_map/reduce_scatter | solution.py:260
  452.7 2.5 fusion.69
  455.2 60.0 %reduce-scatter.7.cloned.1.call-done = bf16[2,256,768]{2,1,0:T(8,128)(2,1)} async-done(((bf16[2,1024,768]{2,1,0:T(8,128)(2,1)}), bf16[2,256,768]{2,1,0:T(8,128)(2,1)}) %reduce-scatter.7.cloned.1.call-update) | async-done | bytes 786448 | tf_op jit(solution)/shard_map/reduce_scatter | solution.py:165
  515.1 4.5 fusion.93
  519.7 63.6 %all-gather.11.cloned.1.call-done = bf16[2,1024,768]{2,1,0:T(8,128)(2,1)} async-done(((bf16[2,256,768]{2,1,0:T(8,128)(2,1)}), bf16[2,1024,768]{2,1,0:T(8,128)(2,1)}) %all-gather.11.cloned.1.call-update) | async-done | bytes 3145744 | tf_op jit(solution)/shard_map/all_gather | solution.py:268
  583.3 3.9 convolution_convert_fusion.2
  590.2 67.5 %while.56 = (s32[]{:T(128)}, bf16[2,1024,192]{1,2,0:T(8,128)(2,1)}, bf16[2,1024,192]{1,2,0:T(8,128)(2,1)}, bf16[2,1024,192]{1,2,0:T(8,128)(2,1)}, bf16[2,1024,3,...) while((s32[]{:T(128)}, bf16[2,1024,192]{1,2,0:T(8,128)(2,1)}, ...), condition=%wide.region_19.20_spmd, body=%wide.region_15.19_spmd.sunk | while | flops 1032321536 | bytes 92443344 | solution.py:278
  591.2 1.9 fusion.137
  597.3 22.5 %while.58 = (s32[]{:T(128)}, f32[1024,3,64]{0,2,1:T(8,128)S(1)}, f32[1024,3,64]{0,2,1:T(8,128)}, bf16[2,512,3,64]{1,3,2,0:T(8,128)(2,1)}, bf16[2,512,3,64]{1,3,2...) while((s32[]{:T(128)}, f32[1024,3,64]{0,2,1:T(8,128)S(1)}, ...), condition=%wide.region_18.18_spmd.clone, body=%wide.region_16.17_spmd.clone.sunk | while | flops 1031928320 | bytes 64086296 | solution.py:103
  600.2 2.0 fusion.149
  602.2 2.5 multiply_reduce_fusion.4
  604.7 1.8 multiply_convert_fusion.3
  611.4 2.0 fusion.149
  613.4 2.5 multiply_reduce_fusion.4
  616.0 1.8 multiply_convert_fusion.3
  624.7 1.9 fusion.137
  630.8 22.5 %while.58 = (s32[]{:T(128)}, f32[1024,3,64]{0,2,1:T(8,128)S(1)}, f32[1024,3,64]{0,2,1:T(8,128)}, bf16[2,512,3,64]{1,3,2,0:T(8,128)(2,1)}, bf16[2,512,3,64]{1,3,2...) while((s32[]{:T(128)}, f32[1024,3,64]{0,2,1:T(8,128)S(1)}, ...), condition=%wide.region_18.18_spmd.clone, body=%wide.region_16.17_spmd.clone.sunk | while | flops 1031928320 | bytes 64086296 | solution.py:103
  633.7 2.0 fusion.149
  635.7 2.5 multiply_reduce_fusion.4
  638.3 1.8 multiply_convert_fusion.3
  644.9 2.0 fusion.149
  647.0 2.5 multiply_reduce_fusion.4
  649.5 1.8 multiply_convert_fusion.3
  657.7 6.2 bitcast_convert_fusion
  664.2 7.1 convolution_bitcast_fusion
  671.3 4.2 convolution_bitcast_fusion.1
  675.5 1.7 convolution_bitcast_fusion.2
  677.2 3.2 fusion.76
  680.6 1.6 convert_reduce_fusion.5
  682.3 40.8 %reduce-scatter.11.cloned.1.call-done = bf16[2,256,768]{2,1,0:T(8,128)(2,1)} async-done(((bf16[2,1024,768]{2,1,0:T(8,128)(2,1)}), bf16[2,256,768]{2,1,0:T(8,128)(2,1)}) %reduce-scatter.11.cloned.1.call-update) | async-done | bytes 786448 | tf_op jit(solution)/shard_map/reduce_scatter | solution.py:294
  723.1 1.8 fusion.61
  724.9 3.0 fusion.70
  728.0 17.7 %all-reduce.2 = (f32[768]{0:T(1024)S(1)}, f32[768]{0:T(1024)S(1)}, f32[768]{0:T(1024)S(1)}, f32[768]{0:T(1024)S(1)}, f32[768]{0:T(1024)S(1)}, /*index=5*/f32[768]{0:T(1024)S(1)}, f32[768]{0:T(1024)S(1)}) all-reduce(f32[768]{0:T(1024)S(1)} %get-tuple-element.284, ...), channel_id=1, replica_groups=mesh['dp'=8,'mp'=4] {'mp'}, use_global_device_ids=true, to_apply=%region_24.25 | all-reduce | flops 5376 | bytes 43008 | tf_op jit(solution)/shard_map/psum | solution.py:311
  745.7 25.3 %all-reduce = (f32[768]{0:T(1024)}, f32[768]{0:T(1024)}, f32[768]{0:T(1024)}, f32[2,192]{1,0:T(2,128)}, f32[768]{0:T(1024)}, /*index=5*/f32[768]{0:T(1024)}, f32[768]{0:T(1024)}, f32[768]{0:T(1024)}, f32[768]{0:T(1024)}) all-reduce(f32[768]{0:T(1024)S(1)} %get-tuple-element.378, ...), channel_id=1, replica_groups=mesh['dp'=8,'mp'=4] {'dp'}, use_global_device_ids=true, to_apply=%region_25.26 | all-reduce | flops 6528 | bytes 52224 | tf_op jit(solution)/shard_map/psum | solution.py:337
  771.0 71.4 %all-reduce.5.cloned.1.call-done = (f32[3,768,192]{1,2,0:T(8,128)}, f32[192,768]{1,0:T(8,128)}, f32[768,768]{1,0:T(8,128)}, f32[768,768]{1,0:T(8,128)}) async-done(((f32[3,768,192]{1,2,0:T(8,128)}, f32[192,768]{1,0:T(8,128)}, f32[768,768]{1,0:T(8,128)}, f32[768,768]{1,0:T(8,128)}), (f32[3,768,192]{1,2,0:T(8,128)}, f32[192,768]{1,0:T(8,128)}, f32[768,768]{1,0:T(8,128)}, ...) | async-done | bytes 7077904 | tf_op jit(solution)/shard_map/psum | solution.py:337
  842.4 2.9 copy.125
  (321 shorter events, 80.8 us)
Async XLA Ops:
  7.2 306.1 %copy-start = (bf16[768,768]{1,0:T(8,128)(2,1)S(1)}, bf16[768,768]{1,0:T(8,128)(2,1)}, u32[]{:S(2)}) copy-start(bf16[768,768]{1,0:T(8,128)(2,1)} %param.37) | copy-start | bytes 3538948
  7.2 6.4 copy-start.49
  7.2 72.7 %all-gather.5.cloned.1.call-start = ((), (), s32[]{:S(2)}) async-start(), calls=%async_computation.4 | async-start | bytes 3932160 | tf_op jit(solution)/shard_map/all_gather | solution.py:133
  8.0 71.9 %copy-start.35 = (pred[2,256]{1,0:T(4,128)(4,1)}, pred[2,256]{1,0:T(4,128)(4,1)S(1)}, u32[]{:S(2)}) copy-start(pred[2,256]{1,0:T(4,128)(4,1)S(1)} %broadcast_compare_fusion.2) | copy-start | bytes 1540
  9.5 70.4 %copy-start.33 = (f32[2,256]{1,0:T(2,128)}, f32[2,256]{1,0:T(2,128)S(1)}, u32[]{:S(2)}) copy-start(f32[2,256]{1,0:T(2,128)S(1)} %broadcast_multiply_fusion.5) | copy-start | bytes 6148
  11.1 68.8 %copy-start.40 = (f32[2,256]{1,0:T(2,128)}, f32[2,256]{1,0:T(2,128)S(1)}, u32[]{:S(2)}) copy-start(f32[2,256]{1,0:T(2,128)S(1)} %add_rsqrt_fusion.1) | copy-start | bytes 6148
  13.6 231.9 %reduce-scatter.5.cloned.1.call-start = ((), (), s32[]{:S(2)}) async-start(), calls=%async_computation.5 | async-start | bytes 7864320 | tf_op jit(solution)/shard_map/reduce_scatter | solution.py:151
  92.5 1.8 copy-start.14
  94.3 2.2 copy-start.28
  101.3 2.2 copy-start.28
  114.5 1.8 copy-start.14
  116.3 2.2 copy-start.28
  121.5 1.8 copy-start.14
  123.3 2.2 copy-start.28
  130.6 5.2 copy-start.4
  135.8 109.6 %copy-start.31 = (f32[768]{0:T(1024)S(1)}, f32[768]{0:T(1024)}, u32[]{:S(2)}) copy-start(f32[768]{0:T(1024)} %param.28) | copy-start | bytes 9220
  135.8 109.6 %copy-start.36 = (pred[2,256]{1,0:T(4,128)(4,1)S(1)}, pred[2,256]{1,0:T(4,128)(4,1)}, u32[]{:S(2)}) copy-start(pred[2,256]{1,0:T(4,128)(4,1)} %copy-done.35) | copy-start | bytes 1540
  135.9 112.0 %copy-start.38 = (f32[768]{0:T(1024)S(1)}, f32[768]{0:T(1024)}, u32[]{:S(2)}) copy-start(f32[768]{0:T(1024)} %param.35) | copy-start | bytes 9220
  135.9 112.0 %copy-start.45 = (f32[768]{0:T(1024)S(1)}, f32[768]{0:T(1024)}, u32[]{:S(2)}) copy-start(f32[768]{0:T(1024)} %param.36) | copy-start | bytes 9220
  135.9 177.3 %all-gather.7.cloned.1.call-start = ((), (), s32[]{:S(2)}) async-start(), calls=%async_computation.6 | async-start | bytes 3932160 | tf_op jit(solution)/shard_map/all_gather | solution.py:154
  249.1 127.8 %all-gather.9.cloned.1.call-start = ((), (), s32[]{:S(2)}) async-start(), calls=%async_computation.8 | async-start | bytes 3932160 | tf_op jit(solution)/shard_map/all_gather | solution.py:243
  249.7 72.6 %copy-start.46 = (f32[768]{0:T(1024)S(1)}, f32[768]{0:T(1024)}, u32[]{:S(2)}) copy-start(f32[768]{0:T(1024)} %param.38) | copy-start | bytes 9220
  249.7 203.0 %reduce-scatter.9.cloned.1.call-start = ((), (), s32[]{:S(2)}) async-start(), calls=%async_computation.9 | async-start | bytes 3932160 | tf_op jit(solution)/shard_map/reduce_scatter | solution.py:260
  319.6 2.7 copy-start.16
  393.6 121.6 %reduce-scatter.7.cloned.1.call-start = ((), (), s32[]{:S(2)}) async-start(), calls=%async_computation.7 | async-start | bytes 3932160 | tf_op jit(solution)/shard_map/reduce_scatter | solution.py:165
  401.0 114.1 %copy-start.18 = (bf16[2,256,768]{2,1,0:T(8,128)(2,1)S(1)}, bf16[2,256,768]{2,1,0:T(8,128)(2,1)}, u32[]{:S(2)}) copy-start(bf16[2,256,768]{2,1,0:T(8,128)(2,1)} %param.41) | copy-start | bytes 2359300
  401.0 114.1 %copy-start.47 = (f32[768]{0:T(1024)S(1)}, f32[768]{0:T(1024)}, u32[]{:S(2)}) copy-start(f32[768]{0:T(1024)} %param.40) | copy-start | bytes 9220
  401.0 182.3 %all-gather.11.cloned.1.call-start = ((), (), s32[]{:S(2)}) async-start(), calls=%async_computation.10 | async-start | bytes 3932160 | tf_op jit(solution)/shard_map/all_gather | solution.py:268
  455.2 128.2 %copy-start.30 = (bf16[192,768]{1,0:T(8,128)(2,1)S(1)}, bf16[192,768]{1,0:T(8,128)(2,1)}, u32[]{:S(2)}) copy-start(bf16[192,768]{1,0:T(8,128)(2,1)} %param.33) | copy-start | bytes 884740
  519.7 203.4 %reduce-scatter.11.cloned.1.call-start = ((), (), s32[]{:S(2)}) async-start(), calls=%async_computation.11 | async-start | bytes 3932160 | tf_op jit(solution)/shard_map/reduce_scatter | solution.py:294
  519.7 70.5 %copy-start.5 = (bf16[2,1024,3,64]{1,3,2,0:T(8,128)(2,1)S(1)}, bf16[2,1024,3,64]{1,3,2,0:T(8,128)(2,1)}, u32[]{:S(2)}) copy-start(bf16[2,1024,3,64]{1,3,2,0:T(8,128)(2,1)} %get-tuple-element.884) | copy-start | bytes 2359300
  590.6 4.9 copy-start.2
  602.2 2.5 copy-start.8
  604.7 1.9 copy-start.10
  613.4 2.5 copy-start.8
  616.0 1.9 copy-start.10
  619.7 4.4 copy-start.3
  624.2 4.9 copy-start.2
  635.7 2.5 copy-start.8
  638.3 1.9 copy-start.10
  647.0 2.5 copy-start.8
  649.5 1.9 copy-start.10
  653.3 4.4 copy-start.3
  664.0 178.4 %all-reduce.5.cloned.1.call-start = ((), (), s32[]{:S(2)}) async-start(), calls=%async_computation.12 | async-start | bytes 14155776 | tf_op jit(solution)/shard_map/psum | solution.py:337
  664.2 7.1 copy-start.51
  664.2 7.1 copy-start.54
  671.3 4.2 copy-start.15
  671.3 4.2 copy-start.19
  671.3 5.9 copy-start.50
  680.4 42.7 %copy-start.6 = (bf16[2,256,768]{2,1,0:T(8,128)(2,1)S(1)}, bf16[2,256,768]{2,1,0:T(8,128)(2,1)}, u32[]{:S(2)}) copy-start(bf16[2,256,768]{2,1,0:T(8,128)(2,1)} %param.25) | copy-start | bytes 2359300
  680.4 42.7 %copy-start.32 = (f32[768]{0:T(1024)S(1)}, f32[768]{0:T(1024)}, u32[]{:S(2)}) copy-start(f32[768]{0:T(1024)} %param.28) | copy-start | bytes 9220
  680.4 42.7 %copy-start.34 = (f32[2,256]{1,0:T(2,128)S(1)}, f32[2,256]{1,0:T(2,128)}, u32[]{:S(2)}) copy-start(f32[2,256]{1,0:T(2,128)} %copy-done.33) | copy-start | bytes 6148
  680.4 42.7 %copy-start.37 = (pred[2,256]{1,0:T(4,128)(4,1)S(1)}, pred[2,256]{1,0:T(4,128)(4,1)}, u32[]{:S(2)}) copy-start(pred[2,256]{1,0:T(4,128)(4,1)} %copy-done.35) | copy-start | bytes 1540
  680.4 42.7 %copy-start.39 = (f32[768]{0:T(1024)S(1)}, f32[768]{0:T(1024)}, u32[]{:S(2)}) copy-start(f32[768]{0:T(1024)} %param.29) | copy-start | bytes 9220
  680.4 42.7 %copy-start.41 = (f32[2,256]{1,0:T(2,128)S(1)}, f32[2,256]{1,0:T(2,128)}, u32[]{:S(2)}) copy-start(f32[2,256]{1,0:T(2,128)} %copy-done.40) | copy-start | bytes 6148
  680.4 44.5 %copy-start.17 = (f32[2,256,768]{2,1,0:T(8,128)S(1)}, f32[2,256,768]{2,1,0:T(8,128)}, u32[]{:S(2)}) copy-start(f32[2,256,768]{2,1,0:T(8,128)} %get-tuple-element.390) | copy-start | bytes 4718596
  682.2 45.7 %copy-start.42 = (f32[768]{0:T(1024)S(1)}, f32[768]{0:T(1024)}, u32[]{:S(2)}) copy-start(f32[768]{0:T(1024)} %get-tuple-element.281) | copy-start | bytes 9220
  682.2 45.7 %copy-start.43 = (f32[768]{0:T(1024)S(1)}, f32[768]{0:T(1024)}, u32[]{:S(2)}) copy-start(f32[768]{0:T(1024)} %get-tuple-element.289) | copy-start | bytes 9220
  682.2 45.7 %copy-start.44 = (f32[768]{0:T(1024)S(1)}, f32[768]{0:T(1024)}, u32[]{:S(2)}) copy-start(f32[768]{0:T(1024)} %get-tuple-element.409) | copy-start | bytes 9220
  682.3 63.5 %copy-start.48 = (f32[768]{0:T(1024)S(1)}, f32[768]{0:T(1024)}, u32[]{:S(2)}) copy-start(f32[768]{0:T(1024)} %get-tuple-element.411) | copy-start | bytes 9220
  842.4 3.0 copy-start.27
  842.4 3.8 copy-start.25
  845.3 2.2 copy-start.24
  846.1 2.8 copy-start.1
  (32 other events, 38.4 us)
Sparse Core Ops, SparseCore 0:
  13.7 66.1 all-gather.4
  136.0 109.4 reduce-scatter.4
  249.2 63.9 all-gather.6
  314.7 62.1 all-gather.8
  393.7 58.9 reduce-scatter.8
  454.8 60.2 reduce-scatter.6
  519.8 63.4 all-gather.10
  664.1 58.9 reduce-scatter.10
  727.9 114.4 all-reduce.4
where the time goes:
time: 865 us; the launch traced here: 856 us
  waiting for transfers between devices  554 us (64%)
  matrix products  107 us (12%)
  local copies, waits for them, and re-layouts  62.7 us (7%)
  other arithmetic  60.6 us (7%)
  blocking collectives  43 us (5%)
  between operations  14.4 us (2%)
  starting transfers between devices  12.4 us (1%)
    reduce_scatter x1, waiting for transfers between devices, forward_pass(): lax.psum_scatter(attention_partial, 'mp', scatter_dimension=1, tiled=True)  110 us
    psum x1, waiting for transfers between devices, body(): lax.psum((w_qkv_grad, qv_bias_grad, w_out_grad, up_weight_grad, up_bias_g...  71.4 us
    all_gather x1, waiting for transfers between devices, forward_pass(): lax.all_gather(first_normalized.astype(jnp.bfloat16), 'mp', axis=1, tiled...  66.1 us
    all_gather x1, waiting for transfers between devices, body(): lax.all_gather(grad_mid.astype(jnp.bfloat16), 'mp', axis=1, tiled=True)  63.6 us
    reduce_scatter x1, waiting for transfers between devices, forward_pass(): lax.psum_scatter(feedforward_partial.astype(jnp.bfloat16), 'mp', scatter_...  60 us
    all_gather x1, waiting for transfers between devices, forward_pass(): lax.all_gather(second_normalized.astype(jnp.bfloat16), 'mp', axis=1, tile...  51.6 us
    reduce_scatter x1, waiting for transfers between devices, body(): lax.psum_scatter(second_partial.astype(jnp.bfloat16), 'mp', scatter_dimen...  51.6 us
    reduce_scatter x1, waiting for transfers between devices, body(): lax.psum_scatter(first_partial.astype(jnp.bfloat16), 'mp', scatter_dimens...  40.8 us
  transfers between devices with their start and end apart: 9, of which 9 were waited for; matrix products, arithmetic and copies ran while one was open for 6% of the time, Pallas kernels for 0%

commit v1 on v0

v1 whole, which is shorter than its diff:
```python
import jax
import jax.numpy as jnp
from jax import lax
from jax.experimental import pallas as pl
from jax.experimental.pallas import tpu as pltpu
from jax.sharding import PartitionSpec as P

HD = 64
EPSILON = 1e-06
NEG_FILL = -1e30
BF = jnp.bfloat16
F32 = jnp.float32
BOTH = ("dp", "mp")
BLOCK_ORDER = (0, 2, 1, 3)
NT = (((1,), (1,)), ((), ()))
NN = (((1,), (0,)), ((), ()))
TN = (((0,), (0,)), ((), ()))


def dot(left, right, dims):
    return lax.dot_general(left, right, dims, preferred_element_type=F32)


def swap_dp(value, bit, dp_size):
    return lax.ppermute(value, "dp", [(i, i ^ bit) for i in range(dp_size)])


def swap_mp(value, bit):
    return lax.ppermute(value, "mp", [(i, i ^ bit) for i in range(4)])


def row_routes(dp_size):
    first, second = [], []
    for pair in range(dp_size // 2):
        for core in range(2):
            for place in range(4):
                source = (2 * pair + core) * 4 + place
                for row in range(2):
                    target = (2 * pair + place // 2) * 4 + 2 * core + row
                    (first if row == place % 2 else second).append((source, target))
    return first, second


def to_rows(first, second, dp_size):
    routes = row_routes(dp_size)
    return (lax.ppermute(first, BOTH, routes[0]), lax.ppermute(second, BOTH, routes[1]))


def from_rows(first, second, dp_size):
    back = [[(target, source) for source, target in route] for route in row_routes(dp_size)]
    return (lax.ppermute(first, BOTH, back[0]), lax.ppermute(second, BOTH, back[1]))


def plane_groups(dp_size):
    return [[base * 8 + core + 2 * k for k in range(4)] for base in range(dp_size // 8) for core in range(2)]


def plane_gather(value, dp_size):
    spread = jnp.broadcast_to(value[None], (4,) + value.shape)
    return lax.all_to_all(spread, "dp", 0, 0, tiled=True, axis_index_groups=plane_groups(dp_size))


def plane_scatter(value, dp_size):
    pieces = lax.all_to_all(value, "dp", 0, 0, tiled=True, axis_index_groups=plane_groups(dp_size))
    return jnp.sum(pieces.astype(F32), axis=0).astype(BF)


def tie(*values):
    return lax.optimization_barrier(values)


def add(left, right):
    return (left.astype(F32) + right.astype(F32)).astype(BF)


def whole(value):
    rank = value.ndim
    return pl.BlockSpec(value.shape, lambda *i: (0,) * rank)


def scalars():
    return pl.BlockSpec(memory_space=pltpu.SMEM)


def call(kernel, name, grid, in_specs, out_specs, out_shape, scratch, flops, moved, args):
    return pl.pallas_call(
        kernel,
        grid=grid,
        in_specs=in_specs,
        out_specs=out_specs,
        out_shape=out_shape,
        scratch_shapes=scratch,
        compiler_params=pltpu.CompilerParams(vmem_limit_bytes=44 << 20),
        cost_estimate=pl.CostEstimate(flops=flops, transcendentals=0, bytes_accessed=moved),
        name=name,
    )(*args)


def centre(rows):
    row_mean = jnp.mean(rows, axis=-1, keepdims=True)
    centred = rows - row_mean
    variance = jnp.mean(centred * centred, axis=-1, keepdims=True)
    inv_scale = lax.rsqrt(variance + EPSILON)
    return (centred * inv_scale, inv_scale)


def centre_back(incoming, unit_rows, inv_scale, gain):
    scaled = incoming * gain
    inner_one = jnp.mean(scaled, axis=-1, keepdims=True)
    inner_two = jnp.mean(scaled * unit_rows, axis=-1, keepdims=True)
    return inv_scale * (scaled - inner_one - unit_rows * inner_two)


def project_kernel(place, one, two, gain, shift, local, near, other, q_bias, v_bias, normed, q, kv, weights):
    strip = one.shape[0]
    for i, rows in enumerate((one, two)):
        unit, _ = centre(rows[...].astype(F32))
        normed[i * strip : (i + 1) * strip] = (unit * gain[...] + shift[...]).astype(BF)
    core = place[0]
    weights[:, 0] = local[...]
    for k in range(4):
        weights[2 * core + k // 2, 1:4, k % 2] = near[k]
        weights[2 - 2 * core + k // 2, 1:4, k % 2] = other[k]
    width = one.shape[1]
    rows = normed[...]
    q[...] = (dot(rows, weights[0].reshape(width, width), NT) + q_bias[...]).astype(BF)
    kv[0] = dot(rows, weights[1].reshape(width, width), NT).astype(BF)
    kv[1] = (dot(rows, weights[2].reshape(width, width), NT) + v_bias[...]).astype(BF)


def project(place, one, two, gain, shift, local, near, other, q_bias, v_bias):
    strip, width = one.shape
    tokens = 2 * strip
    args = (place, one, two, gain, shift, local, near, other, q_bias, v_bias)
    shapes = [
        jax.ShapeDtypeStruct((tokens, width), BF),
        jax.ShapeDtypeStruct((tokens, width), BF),
        jax.ShapeDtypeStruct((2, tokens, width), BF),
        jax.ShapeDtypeStruct((4, 4, 2, width // 8, width), BF),
    ]
    return call(
        project_kernel,
        "project",
        (1,),
        [scalars()] + [whole(x) for x in args[1:]],
        [whole(x) for x in shapes],
        shapes,
        [],
        6 * tokens * width * width,
        12 * width * width,
        args,
    )


def attend_kernel(
    q_ref, own_ref, far_ref, segq_ref, segk_ref, one, two, wo, o_bias, gain, shift,
    ctx_ref, lse_ref, mid_ref, normed_ref, keys, values_t, total,
):
    half = own_ref.shape[1]
    keys[:half] = own_ref[0]
    keys[half:] = far_ref[0]
    values_t[:, :half] = own_ref[1].T
    values_t[:, half:] = far_ref[1].T
    tokens = q_ref.shape[0]
    block = 256
    step = pl.program_id(0)
    for start in range(0, tokens, block):
        span = slice(start, start + block)
        same = segk_ref[...] == segq_ref[:, span]
        query = q_ref[span, :] * jnp.asarray(HD**-0.5, BF)
        lanes = lax.broadcasted_iota(jnp.int32, query.shape, 1)
        pieces = []
        for head in range(2):
            own = (lanes >= HD) if head else (lanes < HD)
            scores = dot(keys[...], jnp.where(own, query, jnp.zeros_like(query)), NT)
            scores = jnp.where(same, scores, NEG_FILL)
            row_max = jnp.max(scores, axis=0, keepdims=True)
            exp_scores = jnp.exp(scores - row_max)
            row_total = jnp.sum(exp_scores, axis=0, keepdims=True)
            part = dot(values_t[head * HD : (head + 1) * HD, :], exp_scores.astype(BF), NN)
            pieces.append(part / row_total)
            lse_ref[0, head : head + 1, span] = row_max + jnp.log(row_total)
        context = jnp.concatenate(pieces, axis=0).T.astype(BF)
        ctx_ref[span, :] = context
        mixed = dot(context, wo[...], NN)

        @pl.when(step == 0)
        def _():
            total[span, :] = mixed

        @pl.when(step > 0)
        def _():
            total[span, :] += mixed

    @pl.when(step == pl.num_programs(0) - 1)
    def _():
        strip = one.shape[0]
        for i, rows in enumerate((one, two)):
            span = slice(i * strip, (i + 1) * strip)
            mid = rows[...].astype(F32) + total[span, :] + o_bias[...]
            mid_ref[span, :] = mid
            unit, _ = centre(mid)
            normed_ref[span, :] = (unit * gain[...] + shift[...]).astype(BF)


def attend(q, own, far, seg_q, seg_k, one, two, wo, o_bias, gain, shift):
    rows, width = q.shape
    pairs = width // 128
    half = own.shape[1]
    args = (q, own, far, seg_q, seg_k, one, two, wo, o_bias, gain, shift)
    head_block = pl.BlockSpec((rows, 128), lambda i: (0, i))
    key_block = pl.BlockSpec((2, half, 128), lambda i: (0, 0, i))
    shapes = [
        jax.ShapeDtypeStruct((rows, width), BF),
        jax.ShapeDtypeStruct((pairs, 2, rows), F32),
        jax.ShapeDtypeStruct((rows, width), F32),
        jax.ShapeDtypeStruct((rows, width), BF),
    ]
    return call(
        attend_kernel,
        "attend",
        (pairs,),
        [head_block, key_block, key_block, whole(seg_q), whole(seg_k), whole(one), whole(two)]
        + [pl.BlockSpec((128, width), lambda i: (3 * pairs + i, 0)), whole(o_bias), whole(gain), whole(shift)],
        [head_block, pl.BlockSpec((1, 2, rows), lambda i: (i, 0, 0)), whole(shapes[2]), whole(shapes[3])],
        shapes,
        [pltpu.VMEM((2 * half, 128), BF), pltpu.VMEM((128, 2 * half), BF), pltpu.VMEM((rows, width), F32)],
        16 * rows * half * width,
        rows * width * 16,
        args,
    )


def load_block(place, flip, at_y, local, first, second, along_x, block):
    piece = local.shape[1]
    core = place[0] if not flip else 1 - place[0]
    for x in range(2):
        spot = place[1 + 2 * at_y + x]
        block[x, 0] = local[core * 4 + spot]
        if along_x:
            block[x, 1:4] = (second if at_y else first)[x]
        else:
            block[x, 1:4] = (second if x else first)[at_y]


def expand_kernel(
    place, normed, mid, bias, local_up, local_down, up0, up1, up2, up3, down0, down1, down2, down3, d_bias,
    active, slope, out, up, down, total,
):
    step = pl.program_id(0)
    ups, downs = (up0, up1, up2, up3), (down0, down1, down2, down3)
    for j in range(4):

        @pl.when(step == j)
        def _():
            g = j - j % 2
            load_block(place, j // 2, j % 2, local_up, ups[g], ups[g + 1], True, up)
            load_block(place, j // 2, j % 2, local_down, downs[g], downs[g + 1], False, down)

    width = normed.shape[1]
    hidden = dot(normed[...], up[...].reshape(width, width), NT) + bias[0]
    cdf = 0.5 * (1.0 + lax.erf(hidden * (0.5**0.5)))
    pulled = cdf + hidden * jnp.exp(-0.5 * hidden * hidden) * 0.3989422804014327
    slope[...] = pulled.astype(BF)
    active[...] = (hidden * cdf).astype(BF)
    part = dot(active[...], down[...].reshape(width, width), NN)

    @pl.when(step == 0)
    def _():
        total[...] = mid[...] + d_bias[...] + part

    @pl.when((step > 0) & (step < 3))
    def _():
        total[...] += part

    @pl.when(step == 3)
    def _():
        out[...] = (total[...] + part).astype(BF)


def expand(place, normed, mid, bias, local_up, local_down, ups, downs, d_bias):
    tokens, width = normed.shape
    piece = width // 8
    args = (place, normed, mid, bias, local_up, local_down, *ups, *downs, d_bias)
    hidden = pl.BlockSpec((tokens, width), lambda j: (0, j))
    shapes = [
        jax.ShapeDtypeStruct((tokens, 4 * width), BF),
        jax.ShapeDtypeStruct((tokens, 4 * width), BF),
        jax.ShapeDtypeStruct((tokens, width), BF),
    ]
    specs = [scalars()] + [whole(x) for x in args[1:]]
    specs[3] = pl.BlockSpec((1, 1, width), lambda j: (j, 0, 0))
    return call(
        expand_kernel,
        "expand",
        (4,),
        specs,
        [hidden, hidden, whole(shapes[2])],
        shapes,
        [pltpu.VMEM((2, 4, piece, width), BF)] * 2 + [pltpu.VMEM((tokens, width), F32)],
        16 * tokens * width * width,
        20 * width * width,
        args,
    )


def expand_back_kernel(
    flip, place, grad, normed, active, slope, local_up, local_down, up0, up1, down0, down1, before,
    up_grad, down_grad, normed_grad, bias_grad, up, down,
):
    step = pl.program_id(0)
    for j in range(2):

        @pl.when(step == j)
        def _():
            load_block(place, flip, j, local_up, up0, up1, True, up)
            load_block(place, flip, j, local_down, down0, down1, False, down)

    width = normed.shape[1]
    wide = up.shape
    incoming = dot(grad[...], down[...].reshape(width, width), NT)
    grad_hidden = (incoming * slope[...].astype(F32)).astype(BF)
    bias_grad[0] = jnp.sum(grad_hidden.astype(F32), axis=0, keepdims=True)
    down_grad[...] = dot(active[...], grad[...], TN).astype(BF).reshape(2, 1, *wide[1:])
    up_grad[0] = dot(grad_hidden, normed[...], TN).astype(BF).reshape(wide)
    part = dot(grad_hidden, up[...].reshape(width, width), NN)

    @pl.when(step == 0)
    def _():
        if before is None:
            normed_grad[...] = part
        else:
            normed_grad[...] = before[...] + part

    @pl.when(step > 0)
    def _():
        normed_grad[...] += part


def expand_back(flip, place, grad, normed, active, slope, local_up, local_down, ups, downs, before):
    tokens, width = normed.shape
    piece = width // 8
    args = (place, grad, normed, active, slope, local_up, local_down, *ups, *downs)
    if before is not None:
        args = args + (before,)

    def kernel(*refs):
        if before is None:
            refs = refs[:11] + (None,) + refs[11:]
        return expand_back_kernel(flip, *refs)

    hidden = pl.BlockSpec((tokens, width), lambda j: (0, j + 2 * flip))
    shapes = [
        jax.ShapeDtypeStruct((2, 2, 4, piece, width), BF),
        jax.ShapeDtypeStruct((2, 2, 4, piece, width), BF),
        jax.ShapeDtypeStruct((tokens, width), F32),
        jax.ShapeDtypeStruct((2, 1, width), F32),
    ]
    specs = [scalars()] + [whole(x) for x in args[1:]]
    specs[3] = specs[4] = hidden
    return call(
        kernel,
        "expand_back_other" if flip else "expand_back_own",
        (2,),
        specs,
        [
            pl.BlockSpec((1, 2, 4, piece, width), lambda j: (j, 0, 0, 0, 0)),
            pl.BlockSpec((2, 1, 4, piece, width), lambda j: (0, j, 0, 0, 0)),
            whole(shapes[2]),
            pl.BlockSpec((1, 1, width), lambda j: (j, 0, 0)),
        ],
        shapes,
        [pltpu.VMEM((2, 4, piece, width), BF)] * 2,
        20 * tokens * width * width,
        16 * width * width,
        args,
    )


def settle_kernel(incoming, mid, grad, gain, wo, grad_mid, grad_attn, grad_context, sums):
    strip = 256
    parts = None
    for at in range(0, mid.shape[0], strip):
        span = slice(at, at + strip)
        unit, inv_scale = centre(mid[span, :])
        given = incoming[span, :]
        outer = grad[span, :].astype(F32)
        made = outer + centre_back(given, unit, inv_scale, gain[...])
        grad_mid[span, :] = made
        grad_attn[span, :] = made.astype(BF)
        grad_context[span, :] = dot(made.astype(BF), wo[...], NT).astype(BF)
        rows = [jnp.sum(v, axis=0, keepdims=True) for v in (made, given * unit, given, outer)]
        parts = rows if parts is None else [a + b for a, b in zip(parts, rows)]
    for i, row in enumerate(parts):
        sums[i : i + 1, :] = row


def settle(incoming, mid, grad, gain, weights):
    tokens, width = mid.shape
    args = (incoming, mid, grad, gain, weights)
    specs = [whole(x) for x in args]
    specs[4] = pl.BlockSpec((width, width), lambda i: (3, 0))
    shapes = [
        jax.ShapeDtypeStruct((tokens, width), F32),
        jax.ShapeDtypeStruct((tokens, width), BF),
        jax.ShapeDtypeStruct((tokens, width), BF),
        jax.ShapeDtypeStruct((8, width), F32),
    ]
    return call(
        settle_kernel,
        "settle",
        (1,),
        specs,
        [whole(x) for x in shapes],
        shapes,
        [],
        2 * tokens * width * width,
        14 * tokens * width,
        args,
    )


def weigh_kernel(flip, place, dq, mine, got, context, normed, grad, out, left, right):
    core = place[0] if not flip else 1 - place[0]
    width = dq.shape[1]
    piece = width // 8

    @pl.when(core == 0)
    def _():
        left[0] = dq[...]
        left[1] = (mine[0].astype(F32) + got[0].astype(F32)).astype(BF)
        right[...] = normed[...]

    @pl.when(core == 1)
    def _():
        left[0] = (mine[1].astype(F32) + got[1].astype(F32)).astype(BF)
        left[1] = context[...]
        right[...] = grad[...]

    for i in range(2):
        rows = normed[...] if i == 0 else right[...]
        made = dot(left[i], rows, TN).astype(BF).reshape(4, 2, piece, width)
        out[2 * i] = made[:, 0]
        out[2 * i + 1] = made[:, 1]


def weigh(flip, place, dq, mine, got, context, normed, grad):
    tokens, width = dq.shape
    args = (place, dq, mine, got, context, normed, grad)
    shape = jax.ShapeDtypeStruct((4, 4, width // 8, width), BF)
    return call(
        lambda *refs: weigh_kernel(flip, *refs),
        "weigh_other" if flip else "weigh_own",
        (1,),
        [scalars()] + [whole(x) for x in args[1:]],
        whole(shape),
        shape,
        [pltpu.VMEM((2, tokens, width), BF), pltpu.VMEM((tokens, width), BF)],
        4 * tokens * width * width,
        8 * width * width,
        args,
    )


def finish_kernel(dq, mine, got, weights, one, two, gain, grad_mid, flags, out_one, out_two, sums, total):
    width = dq.shape[1]
    keys = (mine[0].astype(F32) + got[0].astype(F32)).astype(BF)
    values = (mine[1].astype(F32) + got[1].astype(F32)).astype(BF)
    total[...] = dot(dq[...], weights[0].reshape(width, width), NN)
    total[...] += dot(keys, weights[1].reshape(width, width), NN)
    total[...] += dot(values, weights[2].reshape(width, width), NN)
    strip = one.shape[0]
    gathered = None
    for i, rows in enumerate((one, two)):
        span = slice(i * strip, (i + 1) * strip)
        unit, inv_scale = centre(rows[...].astype(F32))
        incoming = total[span, :]
        grad_start = grad_mid[span, :] + centre_back(incoming, unit, inv_scale, gain[...])
        (out_two if i else out_one)[...] = grad_start.astype(BF)
        masked = jnp.where(flags[span, :] == 1, grad_start, 0.0)
        parts = [jnp.sum(v, axis=0, keepdims=True) for v in (masked, incoming * unit, incoming)]
        gathered = parts if gathered is None else [a + b for a, b in zip(gathered, parts)]
    gathered.append(jnp.sum(dq[...].astype(F32), axis=0, keepdims=True))
    gathered.append(jnp.sum(values.astype(F32), axis=0, keepdims=True))
    for i, row in enumerate(gathered):
        sums[i : i + 1, :] = row


def finish(dq, mine, got, weights, one, two, gain, grad_mid, flags):
    tokens, width = dq.shape
    args = (dq, mine, got, weights, one, two, gain, grad_mid, flags)
    specs = [whole(x) for x in args]
    specs[3] = pl.BlockSpec((3,) + weights.shape[1:], lambda i: (0,) * 5)
    shapes = [
        jax.ShapeDtypeStruct((tokens // 2, width), BF),
        jax.ShapeDtypeStruct((tokens // 2, width), BF),
        jax.ShapeDtypeStruct((8, width), F32),
    ]
    return call(
        finish_kernel,
        "finish",
        (1,),
        specs,
        [whole(x) for x in shapes],
        shapes,
        [pltpu.VMEM((tokens, width), F32)],
        6 * tokens * width * width,
        12 * width * width,
        args,
    )


def attend_back_kernel(
    q_ref,
    own_ref,
    far_ref,
    g_ref,
    ctx_ref,
    lse_ref,
    segq_ref,
    segk_ref,
    dq_ref,
    own_grad_ref,
    far_grad_ref,
    keys,
    keys_t,
    values,
    dk_total,
    dv_total,
):
    half = own_ref.shape[1]
    keys[:half] = own_ref[0]
    keys[half:] = far_ref[0]
    keys_t[:, :half] = own_ref[0].T
    keys_t[:, half:] = far_ref[0].T
    values[:half] = own_ref[1]
    values[half:] = far_ref[1]
    total = q_ref.shape[0]
    block = 256
    scale = jnp.asarray(HD**-0.5, BF)
    for start in range(0, total, block):
        span = slice(start, start + block)
        same = segk_ref[...] == segq_ref[:, span]
        query = q_ref[span, :] * scale
        grad = g_ref[span, :]
        product = (grad.astype(F32) * ctx_ref[span, :].astype(F32)).T
        lanes = lax.broadcasted_iota(jnp.int32, query.shape, 1)
        pieces = []
        for head in range(2):
            own = (lanes >= HD) if head else (lanes < HD)
            query_own = jnp.where(own, query, jnp.zeros_like(query))
            grad_own = jnp.where(own, grad, jnp.zeros_like(grad))
            scores = dot(keys[...], query_own, NT)
            probs = jnp.exp(jnp.where(same, scores, NEG_FILL) - lse_ref[0, head : head + 1, span])
            grad_probs = dot(values[...], grad_own, NT)
            row_dot = jnp.sum(product[head * HD : (head + 1) * HD, :], axis=0, keepdims=True)
            grad_scores = (probs * (grad_probs - row_dot)).astype(BF)
            dv = dot(probs.astype(BF), grad_own, NN)
            dk = dot(grad_scores, query_own, NN)
            if start == 0 and head == 0:
                dv_total[...] = dv
                dk_total[...] = dk
            else:
                dv_total[...] += dv
                dk_total[...] += dk
            pieces.append(dot(keys_t[head * HD : (head + 1) * HD, :], grad_scores, NN))
        dq_ref[span, :] = (jnp.concatenate(pieces, axis=0).T * HD**-0.5).astype(BF)
    own_grad_ref[0] = dk_total[:half].astype(BF)
    far_grad_ref[0] = dk_total[half:].astype(BF)
    own_grad_ref[1] = dv_total[:half].astype(BF)
    far_grad_ref[1] = dv_total[half:].astype(BF)


def attend_back(q, own, far, grad, ctx, lse, seg_q, seg_k):
    rows, width = q.shape
    pairs = width // 128
    half = own.shape[1]
    head_block = pl.BlockSpec((rows, 128), lambda i: (0, i))
    key_block = pl.BlockSpec((2, half, 128), lambda i: (0, 0, i))
    return pl.pallas_call(
        attend_back_kernel,
        grid=(pairs,),
        in_specs=[head_block]
        + [key_block] * 2
        + [
            head_block,
            head_block,
            pl.BlockSpec((1, 2, rows), lambda i: (i, 0, 0)),
            pl.BlockSpec((1, rows), lambda i: (0, 0)),
            pl.BlockSpec((2 * half, 1), lambda i: (0, 0)),
        ],
        out_specs=[head_block] + [key_block] * 2,
        out_shape=[jax.ShapeDtypeStruct((rows, width), BF)]
        + [jax.ShapeDtypeStruct((2, half, width), BF)] * 2,
        scratch_shapes=[
            pltpu.VMEM((2 * half, 128), BF),
            pltpu.VMEM((128, 2 * half), BF),
            pltpu.VMEM((2 * half, 128), BF),
            pltpu.VMEM((2 * half, 128), F32),
            pltpu.VMEM((2 * half, 128), F32),
        ],
        compiler_params=pltpu.CompilerParams(vmem_limit_bytes=40 << 20),
        cost_estimate=pl.CostEstimate(
            flops=10 * rows * 2 * half * width * 2,
            transcendentals=rows * 2 * half * pairs * 2,
            bytes_accessed=rows * width * 24,
        ),
        name="attend_back",
    )(q, own, far, grad, ctx, lse, seg_q, seg_k)


def make_body(dp_size):
    def body(
        tokens,
        segment_ids,
        mask_flags,
        mask_embed,
        first_gain,
        first_shift,
        query_key_value_weight,
        qv_bias,
        output_weight,
        out_bias,
        second_gain,
        second_shift,
        up_weight,
        expand_bias,
        down_weight,
        down_bias,
        out_grad,
    ):
        dp_at = lax.axis_index("dp")
        mp_at = lax.axis_index("mp")
        core = dp_at % 2
        spot = (dp_at // 2) % 4
        parity = mp_at % 2
        width = tokens.shape[2]
        strip = tokens.shape[1]
        piece = width // 8
        place = jnp.stack([core] + [spot ^ r for r in range(4)]).astype(jnp.int32)

        def across(value, bit):
            return swap_dp(value, bit, dp_size)

        def pick(values):
            return (
                lax.dynamic_index_in_dim(values, parity, 0, keepdims=False),
                lax.dynamic_index_in_dim(values, 1 - parity, 0, keepdims=False),
            )

        def row(vector):
            return vector.reshape(1, -1)

        local_attention = jnp.concatenate(
            [query_key_value_weight.transpose(0, 2, 1).reshape(-1, width), output_weight], axis=0
        )
        offset = (core * 4 + spot) * piece
        share_a = lax.dynamic_slice_in_dim(local_attention, offset, piece, 0)
        local_up = up_weight.T
        share_f = jnp.stack(
            [
                lax.dynamic_slice_in_dim(local_up, offset, piece, 0),
                lax.dynamic_slice_in_dim(down_weight, offset, piece, 0),
            ]
        )
        start_rows = jnp.where((mask_flags == 1)[:, :, None], mask_embed.astype(BF), tokens)
        rows_one, rows_two = pick(start_rows)
        grads_one, grads_two = pick(out_grad)
        flags_one, flags_two = pick(mask_flags)
        vectors = jnp.concatenate([qv_bias.reshape(-1), expand_bias])

        def line_of(share, far):
            near = swap_mp(jnp.stack([share, far]), 1)
            return jnp.stack([far, near[0], near[1]])

        far_a = swap_mp(share_a, 2)
        far_a, share_f, rows_one, rows_two = tie(far_a, share_f, rows_one, rows_two)
        line_a = line_of(share_a, far_a)
        far_f = swap_mp(share_f, 2)
        rows_one, rows_two = to_rows(rows_one, rows_two, dp_size)
        line_a, far_f, vectors, segment_ids = tie(line_a, far_f, vectors, segment_ids)
        near_a = plane_gather(line_a, dp_size)
        line_f = line_of(share_f, far_f)
        far_vectors = swap_mp(vectors, 2)
        other_segments = across(segment_ids, 1)
        line_f, far_vectors, rows_one, rows_two, grads_one, grads_two, flags_one, flags_two = tie(
            line_f, far_vectors, rows_one, rows_two, grads_one, grads_two, flags_one, flags_two
        )
        near_vectors = swap_mp(jnp.stack([vectors, far_vectors]), 1)
        line_f, near_a = tie(line_f, near_a)
        other_a = across(near_a, 1)

        row_segments = jnp.where(mp_at // 2 == core, segment_ids, other_segments)
        row_segments = lax.dynamic_index_in_dim(row_segments, parity, 0, keepdims=False)
        quarters = row_segments.reshape(4, strip)

        def quarter(at):
            return lax.dynamic_index_in_dim(quarters, at, 0, keepdims=False)

        own_segments = jnp.concatenate([quarter(2 * core + parity), quarter(2 * core + 1 - parity)])
        far_segments = jnp.concatenate([quarter(2 - 2 * core + parity), quarter(3 - 2 * core - parity)])
        seg_q = own_segments[None, :]
        seg_k = jnp.concatenate([own_segments, far_segments])[:, None]

        vectors = jnp.stack([vectors, far_vectors, near_vectors[0], near_vectors[1]])
        q_width = qv_bias.shape[1]
        q_bias = vectors[:, :q_width].reshape(1, -1)
        v_bias = vectors[:, q_width : 2 * q_width].reshape(1, -1)

        def turn(values, axes):
            for axis, bit in zip(axes, (core, spot // 2, spot % 2)):
                values = jnp.where(bit == 1, jnp.flip(values, axis), values)
            return values

        hidden_bias = turn(vectors[:, 2 * q_width :].reshape(4, 2, 2, 2, piece), (1, 2, 3))
        hidden_bias = hidden_bias.transpose(1, 2, 3, 0, 4).reshape(4, 1, width)

        normed_one, queries, own_kv, weights = project(
            place,
            rows_one,
            rows_two,
            row(first_gain),
            row(first_shift),
            local_attention.reshape(4, 2, piece, width),
            near_a,
            other_a,
            q_bias,
            v_bias,
        )
        flat_weights = weights.reshape(-1, width)
        side_u = across(line_f[:, 0], 2)
        side_d = across(line_f[:, 1], 4)
        far_kv = across(own_kv, 1)
        far_kv, side_u, side_d = tie(far_kv, side_u, side_d)
        first_u = jnp.stack([line_f[:, 0], side_u])
        first_d = jnp.stack([line_f[:, 1], side_d])
        second_u = across(first_u, 4)
        second_d = across(first_d, 2)
        grads_one, grads_two = to_rows(grads_one, grads_two, dp_size)
        flags_one, flags_two = to_rows(flags_one, flags_two, dp_size)
        first_u_far = across(first_u, 1)
        first_d_far = across(first_d, 1)
        context, log_total, mid_rows, normed_two = attend(
            queries,
            own_kv,
            far_kv,
            seg_q,
            seg_k,
            rows_one,
            rows_two,
            flat_weights,
            row(out_bias),
            row(second_gain),
            row(second_shift),
        )
        mid_rows, second_u, second_d, grads_one, grads_two, flags_one, flags_two = tie(
            mid_rows, second_u, second_d, grads_one, grads_two, flags_one, flags_two
        )
        second_u_far = across(second_u, 1)
        second_d_far = across(second_d, 1)
        flags_in = jnp.concatenate([flags_one, flags_two], axis=0)[:, None]
        grads_in = jnp.concatenate([grads_one, grads_two], axis=0)
        ups = (first_u, second_u, first_u_far, second_u_far)
        downs = (first_d, second_d, first_d_far, second_d_far)
        local_up = local_up.reshape(8, piece, width)
        local_down = down_weight.reshape(8, piece, width)
        active, slope, final_rows = expand(
            place, normed_two, mid_rows, hidden_bias, local_up, local_down, ups, downs, row(down_bias)
        )
        back_one, back_two = from_rows(final_rows[:strip], final_rows[strip:], dp_size)

        up_other, down_other, normed_grad, bias_other = expand_back(
            1, place, grads_in, normed_two, active, slope, local_up, local_down, ups[2:], downs[2:], None
        )
        up_got = across(up_other, 1)
        down_got = across(down_other, 1)
        up_own, down_own, normed_grad, bias_own = expand_back(
            0, place, grads_in, normed_two, active, slope, local_up, local_down, ups[:2], downs[:2], normed_grad
        )
        back_one, back_two, normed_grad = tie(back_one, back_two, normed_grad)
        grad_mid, grad_attn, grad_context, sums_two = settle(
            normed_grad, mid_rows, grads_in, row(second_gain), flat_weights
        )
        up_got, down_got, grad_context = tie(up_got, down_got, grad_context)
        up_sent = across(add(up_own[1], up_got[1]), 4)
        down_sent = across(add(down_own[1], down_got[1]), 2)
        up_kept = add(up_own[0], up_got[0])
        down_kept = add(down_own[0], down_got[0])
        dq, own_grad, far_grad = attend_back(
            queries, own_kv, far_kv, grad_context, context, log_total, seg_q, seg_k
        )
        up_sent, down_sent, dq, far_grad = tie(up_sent, down_sent, dq, far_grad)
        got_kv = across(far_grad, 1)
        up_kept = add(up_kept, up_sent)
        down_kept = add(down_kept, down_sent)
        up_sent = across(up_kept[1], 2)
        down_sent = across(down_kept[1], 4)
        attention_other = weigh(1, place, dq, own_grad, got_kv, context, normed_one, grad_attn)
        attention_got = across(attention_other, 1)
        attention_own = weigh(0, place, dq, own_grad, got_kv, context, normed_one, grad_attn)
        up_sent, down_sent, attention_got, attention_own = tie(up_sent, down_sent, attention_got, attention_own)
        pair = jnp.stack([add(up_kept[0], up_sent), add(down_kept[0], down_sent)], axis=1)
        pair_sent = swap_mp(pair[2:], 1)
        attention_grad = plane_scatter(add(attention_own, attention_got), dp_size)
        out_one, out_two, sums_one = finish(
            dq, own_grad, got_kv, weights, rows_one, rows_two, row(first_gain), grad_mid, flags_in
        )
        pair_sent, out_one, out_two, sums_one, bias_own = tie(pair_sent, out_one, out_two, sums_one, bias_own)
        pair = add(pair[:2], pair_sent)
        pair_sent = swap_mp(pair[1], 2)
        start_one, start_two = from_rows(out_one, out_two, dp_size)

        def placed(values):
            values = jnp.stack([values[i] for i in (0, 2, 1, 3)]).reshape(2, 2, -1)
            for axis, bit in ((0, mp_at // 2), (1, mp_at % 2)):
                values = jnp.where(bit == 1, jnp.flip(values, axis), values)
            return values.reshape(4, -1)

        hidden_sum = jnp.concatenate([bias_own, bias_other]).reshape(2, 2, 2, 4, piece)
        hidden_sum = turn(hidden_sum.transpose(3, 0, 1, 2, 4), (1, 2, 3)).reshape(4, width)
        qv_sum = jnp.concatenate([sums_one[3].reshape(4, -1), sums_one[4].reshape(4, -1)], axis=1)
        small = jnp.concatenate(
            [sums_one[:3], sums_two[:4], placed(qv_sum).reshape(2, width), placed(hidden_sum)], axis=0
        )
        bits = [1 << n for n in range(dp_size.bit_length() - 1)]
        for bit in bits[:2]:
            small = small + across(small, bit)
        pair_sent, attention_grad, small = tie(pair_sent, attention_grad, small)
        attention_sent = swap_mp(attention_grad[2:], 1)

        def gather_back(value):
            for bit in bits[3:]:
                value = value + across(value, bit)
            near = plane_gather(value, dp_size)
            other = across(near, 1)
            return jnp.stack([jnp.where(core == 0, near, other), jnp.where(core == 0, other, near)])

        for bit in bits[2:]:
            small = small + across(small, bit)
        attention_sent, pair, small = tie(attention_sent, pair, small)
        pair = gather_back(add(pair[0], pair_sent))
        attention_grad = add(attention_grad[:2], attention_sent)
        attention_sent = swap_mp(attention_grad[1], 2)
        for bit in (1, 2):
            small = small + swap_mp(small, bit)
        attention_grad = gather_back(add(attention_grad[0], attention_sent)).reshape(4, 2 * piece, width)

        activations = jnp.where(
            parity == 0, jnp.stack([back_one, back_two]), jnp.stack([back_two, back_one])
        )
        grad_start = jnp.where(
            parity == 0, jnp.stack([start_one, start_two]), jnp.stack([start_two, start_one])
        )
        tokens_grad = jnp.where((mask_flags == 1)[:, :, None], 0.0, grad_start.astype(F32))
        up_weight_grad = pair[:, :, 0].reshape(width, width).astype(F32).T
        down_weight_grad = pair[:, :, 1].reshape(width, width).astype(F32)
        w_qkv_grad = attention_grad[:3].astype(F32).transpose(0, 2, 1)
        w_out_grad = attention_grad[3].astype(F32)
        qv_bias_grad = lax.dynamic_index_in_dim(small[7:9].reshape(4, 2, -1), mp_at, 0, keepdims=False)
        up_bias_grad = lax.dynamic_index_in_dim(small[9:13], mp_at, 0, keepdims=False)
        return (
            activations,
            tokens_grad,
            small[0],
            small[1],
            small[2],
            w_qkv_grad,
            qv_bias_grad,
            w_out_grad,
            small[3],
            small[4],
            small[5],
            up_weight_grad,
            up_bias_grad,
            down_weight_grad,
            small[6],
        )

    return body


def solution(mesh):
    in_specs = (
        P("dp", "mp", None),
        P("dp", None),
        P("dp", "mp"),
        P(),
        P(),
        P(),
        P(None, None, "mp"),
        P(None, "mp"),
        P("mp", None),
        P(),
        P(),
        P(),
        P(None, "mp"),
        P("mp"),
        P("mp", None),
        P(),
        P("dp", "mp", None),
    )
    out_specs = (
        P("dp", "mp", None),
        P("dp", "mp", None),
        P(),
        P(),
        P(),
        P(None, None, "mp"),
        P(None, "mp"),
        P("mp", None),
        P(),
        P(),
        P(),
        P(None, "mp"),
        P("mp"),
        P("mp", None),
        P(),
    )
    return jax.shard_map(
        make_body(mesh.shape["dp"]), mesh=mesh, in_specs=in_specs, out_specs=out_specs, check_vma=False
    )
```

time: 865 us -> 385 us (0.45)
  waiting for transfers between devices: 554 us -> 103 us
  matrix products: 107 us -> 0 us
  Pallas kernels: 0 us -> 97.7 us
  starting transfers between devices: 12.4 us -> 97.1 us
  blocking collectives: 43 us -> 0 us
  other arithmetic: 60.6 us -> 32.3 us
  local copies, waits for them, and re-layouts: 62.7 us -> 45.7 us
  between operations: 14.4 us -> 2.42 us
    reduce_scatter x4 -> x0, waiting for transfers between devices: 262 us -> none  [the longest x1 110 us: forward_pass(): lax.psum_scatter(attention_partial, 'mp', scatter_dimension=1, tiled=True)]
    all_gather x4 -> x0, waiting for transfers between devices: 220 us -> none  [the longest x1 66.1 us: forward_pass(): lax.all_gather(first_normalized.astype(jnp.bfloat16), 'mp', axis=1, tiled...]
    dot_general x40 -> x0, matrix products: 107 us -> none  [the longest x1 11.1 us: body(): jnp.einsum('xku,qu->xkq', complete_grad, down_weight, preferred_element_t...]
    pallas_call x0 -> x10, Pallas kernels: none -> 97.7 us  [the longest x9 78.8 us: call(): pl.pallas_call(kernel, grid=grid, in_specs=in_specs, out_specs=out_specs,...]
    ppermute x0 -> x46, waiting for transfers between devices: none -> 97.3 us  [the longest x24 49.4 us: swap_dp(): return lax.ppermute(value, 'dp', [(i, i ^ bit) for i in range(dp_size)])]
    ppermute x0 -> x46, starting transfers between devices: none -> 82.5 us  [the longest x24 46.9 us: swap_dp(): return lax.ppermute(value, 'dp', [(i, i ^ bit) for i in range(dp_size)])]
    psum x1 -> x0, waiting for transfers between devices: 71.4 us -> none  [body(): lax.psum((w_qkv_grad, qv_bias_grad, w_out_grad, up_weight_grad, up_bias_g...]
    psum x2 -> x0, blocking collectives: 43 us -> none  [the longest x1 25.3 us: body(): lax.psum((w_qkv_grad, qv_bias_grad, w_out_grad, up_weight_grad, up_bias_g...]
  transfers between devices with their start and end apart: 9 -> 50, of which waited for: 9 -> 23; matrix products, arithmetic and copies ran while one was open for 6% -> 10% of each run, Pallas kernels for 0% -> 17%
where the time goes in v1:
time: 385 us; the launch traced here: 378 us
  waiting for transfers between devices  103 us (27%)
  Pallas kernels  97.7 us (25%)
  starting transfers between devices  97.1 us (25%)
  local copies, waits for them, and re-layouts  45.7 us (12%)
  other arithmetic  32.3 us (8%)
    pallas_call x9, Pallas kernels, call(): pl.pallas_call(kernel, grid=grid, in_specs=in_specs, out_specs=out_specs,...  78.8 us
    ppermute x24, waiting for transfers between devices, swap_dp(): return lax.ppermute(value, 'dp', [(i, i ^ bit) for i in range(dp_size)])  49.4 us
    ppermute x12, waiting for transfers between devices, swap_mp(): return lax.ppermute(value, 'mp', [(i, i ^ bit) for i in range(4)])  47.9 us
    ppermute x24, starting transfers between devices, swap_dp(): return lax.ppermute(value, 'dp', [(i, i ^ bit) for i in range(dp_size)])  46.9 us
    unnamed x154, local copies, waits for them, and re-layouts  28.1 us
    ppermute x12, starting transfers between devices, swap_mp(): return lax.ppermute(value, 'mp', [(i, i ^ bit) for i in range(4)])  22.5 us
    pallas_call x1, Pallas kernels, attend_back(): pl.pallas_call(attend_back_kernel, grid=(pairs,), in_specs=[head_block] +...  18.9 us
    convert_element_type x9, other arithmetic, add(): return (left.astype(F32) + right.astype(F32)).astype(BF)  11.4 us
  transfers between devices with their start and end apart: 50, of which 23 were waited for; matrix products, arithmetic and copies ran while one was open for 10% of the time, Pallas kernels for 17%

profile of v1, /device:TPU:0, one launch (start us, length us, event | category | flops | bytes accessed | tf_op | source)
XLA Modules:
  0.0 378.4 jit_solution(11679402512847564270)
XLA Ops:
  1.8 4.1 %collective-permute-start = (bf16[96,768]{1,0:T(8,128)(2,1)S(1)}, bf16[96,768]{1,0:T(8,128)(2,1)S(1)}, u32[]{:S(2)}, u32[]{:S(2)}) collective-permute-start(bf16[96,768]{1,0:T(8,128)(2,1)S(1)} %fusion.15), channel_id=1, source_target_pairs={{0,2},{1,3},{2,0},{3,1},{4,6},{5,7},{6,4},{7,5},{8,10},{9,11},{10,... | collective-permute-start | bytes 442376 | tf_op jit(solution)/shard_map/ppermute | solution.py:29
  9.3 3.6 collective-permute-done
  13.7 3.4 collective-permute-start.2
  17.2 10.1 %collective-permute-done.1 = bf16[2,96,768]{2,1,0:T(8,128)(2,1)S(1)} collective-permute-done((bf16[2,96,768]{2,1,0:T(8,128)(2,1)S(1)}, bf16[2,96,768]{2,1,0:T(8,128)(2,1)S(1)}, u32[]{:S(2)}, u32[]{:S(2)}) %collective-permute-start.1) | collective-permute-done | bytes 294944 | tf_op jit(solution)/shard_map/ppermute | solution.py:29
  27.3 3.0 collective-permute-done.2
  31.7 3.7 all-to-all-start
  35.9 1.6 collective-permute-start.5
  37.6 1.7 collective-permute-start.6
  40.2 2.6 collective-permute-start.4
  42.9 10.3 %collective-permute-done.3 = bf16[2,2,96,768]{3,2,0,1:T(8,128)(2,1)S(1)} collective-permute-done((bf16[2,2,96,768]{3,2,0,1:T(8,128)(2,1)S(1)}, bf16[2,2,96,768]{3,2,0,1:T(8,128)(2,1)S(1)}, u32[]{:S(2)}, u32[]{:S(2)}) %collective-permute-start.3) | collective-permute-done | bytes 589856 | tf_op jit(solution)/shard_map/ppermute | solution.py:29
  54.1 4.2 %collective-permute-done.4 = f32[1152]{0:T(1024)S(1)} collective-permute-done((f32[1152]{0:T(1024)S(1)}, f32[1152]{0:T(1024)S(1)}, u32[]{:S(2)}, u32[]{:S(2)}) %collective-permute-start.4) | collective-permute-done | bytes 4640 | tf_op jit(solution)/shard_map/ppermute | solution.py:29
  59.1 4.8 %collective-permute-start.7 = (bf16[4,3,96,768]{3,2,1,0:T(8,128)(2,1)S(1)}, bf16[4,3,96,768]{3,2,1,0:T(8,128)(2,1)}, u32[]{:S(2)}, u32[]{:S(2)}) collective-permute-start(bf16[4,3,96,768]{3,2,1,0:T(8,128)(2,1)S(1)} %all-to-all-done.near), channel_id=1, source_target_pairs={{0,4},{4,0},{8,12},{12,8},{16,20},{20,16},{24,28},{28,24},{1,5},{5... | collective-permute-start | bytes 5308424 | tf_op jit(solution)/shard_map/ppermute | solution.py:25
  68.9 4.2 %project.1 = (bf16[512,768]{1,0:T(8,128)(2,1)S(1)}, bf16[512,768]{1,0:T(8,128)(2,1)S(1)}, bf16[2,512,768]{2,1,0:T(8,128)(2,1)S(1)}, bf16[4,4,2,96,768]{4,3,2,1,0:T(8,128)(2,1)}) custom-call(s32[5]{0:T(128)S(1)} %stack.148.place.refs_0_, bf16[256,768]{1,0:T(8,128)(2,1)S(1)} %collective-permute-done.5.one, bf16[256,768]{1,0:T(8,128)(2,1)S(1)} %copy-done.23, ...), custom_call_target="tpu_custom_call" | custom-call | flops 1811939328 | bytes 7077888 | tf_op jit(solution)/shard_map/project/pallas_call | solution.py:86
  75.4 1.7 collective-permute-start.10
  77.1 1.5 collective-permute-start.11
  78.5 8.7 %collective-permute-done.10 = bf16[3,96,768]{2,1,0:T(8,128)(2,1)S(1)} collective-permute-done((bf16[3,96,768]{2,1,0:T(8,128)(2,1)S(1)}, bf16[3,96,768]{2,1,0:T(8,128)(2,1)S(1)}, u32[]{:S(2)}, u32[]{:S(2)}) %collective-permute-start.10) | collective-permute-done | bytes 442400 | tf_op jit(solution)/shard_map/ppermute | solution.py:25
  88.8 1.5 collective-permute-start.13
  92.0 1.6 copy.53
  94.8 4.5 %collective-permute-start.15 = (bf16[256,768]{1,0:T(8,128)(2,1)}, bf16[256,768]{1,0:T(8,128)(2,1)}, u32[]{:S(2)}, u32[]{:S(2)}) collective-permute-start(bf16[256,768]{1,0:T(8,128)(2,1)} %get-tuple-element.119), channel_id=1, source_target_pairs={{0,0},{1,1},{2,4},{3,5},{4,2},{5,3},{6,6},{7,7},{8,8},{9,9},{10,12... | collective-permute-start | bytes 1179656 | tf_op jit(solution)/shard_map/ppermute | solution.py:46
  104.4 1.4 copy-done.28
  105.8 1.4 copy-done.31
  108.3 25.4 %attend.1 = (bf16[512,768]{1,0:T(8,128)(2,1)S(1)}, f32[6,2,512]{2,1,0:T(2,128)S(1)}, f32[512,768]{1,0:T(8,128)S(1)}, bf16[512,768]{1,0:T(8,128)(2,1)S(1)}) custom-call(bf16[512,768]{1,0:T(8,128)(2,1)S(1)} %copy-done.38, bf16[2,512,768]{2,1,0:T(8,128)(2,1)S(1)} %copy-done.28, bf16[2,512,768]{2,1,0:T(8,128)(2,1)S(1)} %copy-done.31, s32[1,512]{1,0:T(1,128)S(1)} %bitcast.144, ...), custom_call_target="tpu_custom_call" | custom-call | flops 3221225472 | bytes 6291456 | tf_op jit(solution)/shard_map/attend/pallas_call | solution.py:86
  135.8 17.4 %collective-permute-start.19 = (bf16[2,3,96,768]{3,2,1,0:T(8,128)(2,1)S(1)}, bf16[2,3,96,768]{3,2,1,0:T(8,128)(2,1)}, u32[]{:S(2)}, u32[]{:S(2)}) collective-permute-start(bf16[2,3,96,768]{3,2,1,0:T(8,128)(2,1)S(1)} %pad_maximum_fusion.4.up0.refs_7_), channel_id=1, source_target_pairs={{0,4},{4,0},{8,12},{12,8},{16,20},{20,16},{24,28},{28,24},{1,5},{5... | collective-permute-start | bytes 2654216 | tf_op jit(solution)/shard_map/ppermute | solution.py:25
  159.3 14.3 %expand.1 = (bf16[512,3072]{1,0:T(8,128)(2,1)}, bf16[512,3072]{1,0:T(8,128)(2,1)}, bf16[512,768]{1,0:T(8,128)(2,1)S(1)}) custom-call(s32[5]{0:T(128)S(1)} %stack.148.place.refs_0_, bf16[512,768]{1,0:T(8,128)(2,1)S(1)} %copy-done.41, f32[512,768]{1,0:T(8,128)} %copy-done.13, f32[4,1,768]{2,1,0:T(1,128)S(1)} %reshape.158.bias, ...), custom_call_target="tpu_custom_call" | custom-call | flops 4831838208 | bytes 11796480 | tf_op jit(solution)/shard_map/expand/pallas_call | solution.py:86
  173.6 9.9 %expand_back_other.1 = (bf16[2,2,4,96,768]{4,3,2,1,0:T(8,128)(2,1)}, bf16[2,2,4,96,768]{4,3,2,1,0:T(8,128)(2,1)}, f32[512,768]{1,0:T(8,128)S(1)}, f32[2,1,768]{2,1,0:T(1,128)S(1)}) custom-call(s32[5]{0:T(128)S(1)} %stack.148.place.refs_0_, bf16[512,768]{1,0:T(8,128)(2,1)S(1)} %constant_dynamic-update-slice_fusion.refs_1_.grad, ...), custom_call_target="tpu_custom_call" | custom-call | flops 6039797760 | bytes 9437184 | tf_op jit(solution)/shard_map/expand_back_other/pallas_call | solution.py:86
  185.2 10.3 %expand_back_own.1 = (bf16[2,2,4,96,768]{4,3,2,1,0:T(8,128)(2,1)}, bf16[2,2,4,96,768]{4,3,2,1,0:T(8,128)(2,1)}, f32[512,768]{1,0:T(8,128)S(1)}, f32[2,1,768]{2,1,0:T(1,128)S(1)}) custom-call(s32[5]{0:T(128)S(1)} %stack.148.place.refs_0_, bf16[512,768]{1,0:T(8,128)(2,1)S(1)} %constant_dynamic-update-slice_fusion.refs_1_.grad, ...), custom_call_target="tpu_custom_call" | custom-call | flops 6039797760 | bytes 9437184 | tf_op jit(solution)/shard_map/expand_back_own/pallas_call | solution.py:86
  196.3 3.3 settle.1
  199.7 2.4 fusion.3
  202.8 1.7 collective-permute-start.28
  204.6 18.9 %attend_back.1 = (bf16[512,768]{1,0:T(8,128)(2,1)S(1)}, bf16[2,512,768]{2,1,0:T(8,128)(2,1)S(1)}, bf16[2,512,768]{2,1,0:T(8,128)(2,1)S(1)}) custom-call(bf16[512,768]{1,0:T(8,128)(2,1)S(1)} %copy-done.39, bf16[2,512,768]{2,1,0:T(8,128)(2,1)S(1)} %copy-done.29, bf16[2,512,768]{2,1,0:T(8,128)(2,1)S(1)} %copy-done.32, ...), custom_call_target="tpu_custom_call" | custom-call | flops 8053063680 | bytes 9437184 | tf_op jit(solution)/shard_map/attend_back/pallas_call | solution.py:580
  225.8 5.8 %collective-permute-start.31 = (bf16[2,512,768]{2,1,0:T(8,128)(2,1)S(1)}, bf16[2,512,768]{2,1,0:T(8,128)(2,1)S(1)}, u32[]{:S(2)}, u32[]{:S(2)}) collective-permute-start(bf16[2,512,768]{2,1,0:T(8,128)(2,1)S(1)} %get-tuple-element.152), channel_id=1, source_target_pairs={{0,4},{4,0},{8,12},{12,8},{16,20},{20,16},{24,28},{28,24},{1,5},{5... | collective-permute-start | bytes 4718600 | tf_op jit(solution)/shard_map/ppermute | solution.py:25
  231.6 3.0 collective-permute-done.31.refs_3_.got
  235.8 3.6 weigh_other.1
  239.8 1.9 fusion.1
  242.6 1.7 collective-permute-start.29
  246.0 1.5 collective-permute-start.30
  252.1 2.5 weigh_own.1
  254.6 3.8 collective-permute-done.29
  258.3 3.1 collective-permute-done.30
  261.5 1.6 fusion.9
  264.0 3.4 collective-permute-start.33
  268.7 1.4 copy-done.16
  272.1 5.2 %finish.1 = (bf16[256,768]{1,0:T(8,128)(2,1)S(1)}, bf16[256,768]{1,0:T(8,128)(2,1)S(1)}, f32[8,768]{1,0:T(8,128)S(1)}) custom-call(bf16[512,768]{1,0:T(8,128)(2,1)S(1)} %copy-done.4, bf16[2,512,768]{2,1,0:T(8,128)(2,1)S(1)} %get-tuple-element.151.refs_2_.mine, bf16[2,512,768]{2,1,0:T(8,128)(2,1)S(1)} %collective-permute-done.31.refs_3_.got, ...), custom_call_target="tpu_custom_call" | custom-call | flops 1811939328 | bytes 7077888 | tf_op jit(solution)/shard_map/finish/pallas_call | solution.py:86
  278.9 3.8 %add_convert_fusion = bf16[4,4,96,768]{3,2,1,0:T(8,128)(2,1)} fusion(bf16[4,4,96,768]{3,2,1,0:T(8,128)(2,1)} %collective-permute-done.32, bf16[4,4,96,768]{3,2,1,0:T(8,128)(2,1)S(1)} %copy-done.1), kind=kLoop, calls=%fused_computation | loop fusion | flops 4718592 | bytes 7077888 | tf_op jit(solution)/shard_map/convert_element_type | solution.py:73
  282.7 3.8 all-to-all-start.1
  291.2 2.0 collective-permute-start.38
  293.2 21.1 %collective-permute-done.38 = f32[13,768]{1,0:T(8,128)S(1)} collective-permute-done((f32[13,768]{1,0:T(8,128)S(1)}, f32[13,768]{1,0:T(8,128)S(1)}, u32[]{:S(2)}, u32[]{:S(2)}) %collective-permute-start.38) | collective-permute-done | bytes 39968 | tf_op jit(solution)/shard_map/ppermute | solution.py:25
  316.2 1.5 collective-permute-start.40
  317.6 2.8 collective-permute-done.40
  320.5 1.4 add.155
  322.5 2.5 collective-permute-start.43
  325.0 5.2 %collective-permute-done.43 = bf16[96,768]{1,0:T(8,128)(2,1)S(1)} collective-permute-done((bf16[96,768]{1,0:T(8,128)(2,1)S(1)}, bf16[96,768]{1,0:T(8,128)(2,1)S(1)}, u32[]{:S(2)}, u32[]{:S(2)}) %collective-permute-start.43) | collective-permute-done | bytes 147488 | tf_op jit(solution)/shard_map/ppermute | solution.py:29
  331.1 3.5 all-to-all-start.2
  335.6 5.9 %all-to-all-done.2 = bf16[4,96,768]{2,1,0:T(8,128)(2,1)S(1)} async-done(((bf16[4,96,768]{2,1,0:T(8,128)(2,1)}), bf16[4,96,768]{2,1,0:T(8,128)(2,1)S(1)}, u32[]{:S(2)}, u32[]{:S(2)}) %all-to-all-start.2) | async-done | bytes 589856 | tf_op jit(solution)/shard_map/all_to_all | solution.py:60
  342.6 3.7 all-to-all-start.3
  347.8 2.0 collective-permute-start.41
  349.8 1.8 collective-permute-start.44
  351.6 2.4 maximum_select_fusion
  354.0 5.5 %collective-permute-done.41 = f32[13,768]{1,0:T(8,128)S(1)} collective-permute-done((f32[13,768]{1,0:T(8,128)}, f32[13,768]{1,0:T(8,128)S(1)}, u32[]{:S(2)}, u32[]{:S(2)}) %collective-permute-start.41) | collective-permute-done | bytes 39968 | tf_op jit(solution)/shard_map/ppermute | solution.py:29
  361.1 2.5 convert_select_fusion
  363.6 4.3 %collective-permute-done.42 = f32[13,768]{1,0:T(8,128)S(1)} collective-permute-done((f32[13,768]{1,0:T(8,128)S(1)}, f32[13,768]{1,0:T(8,128)S(1)}, u32[]{:S(2)}, u32[]{:S(2)}) %collective-permute-start.42) | collective-permute-done | bytes 39968 | tf_op jit(solution)/shard_map/ppermute | solution.py:29
  368.6 1.4 collective-permute-start.45
  374.3 2.0 copy.62
  376.3 1.7 bitcast_convert_fusion
  (324 shorter events, 73.6 us)
Async XLA Ops:
  0.7 7.4 %copy-start.55 = (bf16[2,256,768]{2,1,0:T(8,128)(2,1)S(1)}, bf16[2,256,768]{2,1,0:T(8,128)(2,1)}, u32[]{:S(2)}) copy-start(bf16[2,256,768]{2,1,0:T(8,128)(2,1)} %param.17) | copy-start | bytes 2359300
  1.8 11.1 %collective-permute-start = (bf16[96,768]{1,0:T(8,128)(2,1)S(1)}, bf16[96,768]{1,0:T(8,128)(2,1)S(1)}, u32[]{:S(2)}, u32[]{:S(2)}) collective-permute-start(bf16[96,768]{1,0:T(8,128)(2,1)S(1)} %fusion.15), channel_id=1, source_target_pairs={{0,2},{1,3},{2,0},{3,1},{4,6},{5,7},{6,4},{7,5},{8,10},{9,11},{10,... | collective-permute-start | bytes 442376 | tf_op jit(solution)/shard_map/ppermute | solution.py:29
  8.3 8.8 %copy-start.74 = (f32[2,192]{1,0:T(2,128)S(1)}, f32[2,192]{1,0:T(2,128)}, u32[]{:S(2)}) copy-start(f32[2,192]{1,0:T(2,128)} %param.24) | copy-start | bytes 4612
  8.3 8.9 %copy-start.65 = (f32[768]{0:T(1024)S(1)}, f32[768]{0:T(1024)}, u32[]{:S(2)}) copy-start(f32[768]{0:T(1024)} %param.30) | copy-start | bytes 9220
  12.9 14.4 %collective-permute-start.1 = (bf16[2,96,768]{2,1,0:T(8,128)(2,1)S(1)}, bf16[2,96,768]{2,1,0:T(8,128)(2,1)S(1)}, u32[]{:S(2)}, u32[]{:S(2)}) collective-permute-start(bf16[2,96,768]{2,1,0:T(8,128)(2,1)S(1)} %pad_maximum_fusion.10), channel_id=1, source_target_pairs={{0,1},{1,0},{2,3},{3,2},{4,5},{5,4},{6,7},{7,6},{8,9},{9,8},{10,11... | collective-permute-start | bytes 884744 | tf_op jit(solution)/shard_map/ppermute | solution.py:29
  13.7 16.7 %collective-permute-start.2 = (bf16[2,96,768]{2,1,0:T(8,128)(2,1)S(1)}, bf16[2,96,768]{2,1,0:T(8,128)(2,1)S(1)}, u32[]{:S(2)}, u32[]{:S(2)}) collective-permute-start(bf16[2,96,768]{2,1,0:T(8,128)(2,1)S(1)} %pad_maximum_fusion.9), channel_id=1, source_target_pairs={{0,2},{1,3},{2,0},{3,1},{4,6},{5,7},{6,4},{7,5},{8,10},{9,11},{10,... | collective-permute-start | bytes 884744 | tf_op jit(solution)/shard_map/ppermute | solution.py:29
  31.7 27.4 %all-to-all-start = ((bf16[4,3,96,768]{3,2,1,0:T(8,128)(2,1)}), bf16[4,3,96,768]{3,2,1,0:T(8,128)(2,1)S(1)}, u32[]{:S(2)}, u32[]{:S(2)}) async-start(bf16[4,3,96,768]{3,2,1,0:T(8,128)(2,1)} %broadcast_in_dim.53), calls=%async_computation | async-start | bytes 3538944 | tf_op jit(solution)/shard_map/all_to_all | solution.py:60
  35.5 17.6 %collective-permute-start.3 = (bf16[2,2,96,768]{3,2,0,1:T(8,128)(2,1)S(1)}, bf16[2,2,96,768]{3,2,0,1:T(8,128)(2,1)S(1)}, u32[]{:S(2)}, u32[]{:S(2)}) collective-permute-start(bf16[2,2,96,768]{3,2,0,1:T(8,128)(2,1)S(1)} %pad_maximum_fusion.7), channel_id=1, source_target_pairs={{0,1},{1,0},{2,3},{3,2},{4,5},{5,4},{6,7},{7,6},{8,9},{9,8},{10,11... | collective-permute-start | bytes 1769480 | tf_op jit(solution)/shard_map/ppermute | solution.py:29
  35.9 22.4 %collective-permute-start.5 = (bf16[256,768]{1,0:T(8,128)(2,1)}, bf16[256,768]{1,0:T(8,128)(2,1)S(1)}, u32[]{:S(2)}, u32[]{:S(2)}) collective-permute-start(bf16[256,768]{1,0:T(8,128)(2,1)} %get-tuple-element.101), channel_id=1, source_target_pairs={{0,0},{1,1},{2,4},{3,5},{4,2},{5,3},{6,6},{7,7},{8,8},{9,9},{10,12... | collective-permute-start | bytes 1179656 | tf_op jit(solution)/shard_map/ppermute | solution.py:46
  37.6 20.7 %collective-permute-start.6 = (bf16[256,768]{1,0:T(8,128)(2,1)S(1)}, bf16[256,768]{1,0:T(8,128)(2,1)S(1)}, u32[]{:S(2)}, u32[]{:S(2)}) collective-permute-start(bf16[256,768]{1,0:T(8,128)(2,1)S(1)} %copy-done.59), channel_id=1, source_target_pairs={{0,1},{1,0},{2,5},{3,4},{4,3},{5,2},{6,7},{7,6},{8,9},{9,8},{10,13... | collective-permute-start | bytes 1179656 | tf_op jit(solution)/shard_map/ppermute | solution.py:46
  40.2 18.1 %collective-permute-start.4 = (f32[1152]{0:T(1024)S(1)}, f32[1152]{0:T(1024)S(1)}, u32[]{:S(2)}, u32[]{:S(2)}) collective-permute-start(f32[1152]{0:T(1024)S(1)} %pad_maximum_fusion.16), channel_id=1, source_target_pairs={{0,2},{1,3},{2,0},{3,1},{4,6},{5,7},{6,4},{7,5},{8,10},{9,11},{10,... | collective-permute-start | bytes 13832 | tf_op jit(solution)/shard_map/ppermute | solution.py:29
  58.3 9.6 %copy-start.19 = (bf16[256,768]{1,0:T(8,128)(2,1)}, bf16[256,768]{1,0:T(8,128)(2,1)S(1)}, u32[]{:S(2)}) copy-start(bf16[256,768]{1,0:T(8,128)(2,1)S(1)} %collective-permute-done.5.one) | copy-start | bytes 1179652
  59.1 8.8 %collective-permute-start.7 = (bf16[4,3,96,768]{3,2,1,0:T(8,128)(2,1)S(1)}, bf16[4,3,96,768]{3,2,1,0:T(8,128)(2,1)}, u32[]{:S(2)}, u32[]{:S(2)}) collective-permute-start(bf16[4,3,96,768]{3,2,1,0:T(8,128)(2,1)S(1)} %all-to-all-done.near), channel_id=1, source_target_pairs={{0,4},{4,0},{8,12},{12,8},{16,20},{20,16},{24,28},{28,24},{1,5},{5... | collective-permute-start | bytes 5308424 | tf_op jit(solution)/shard_map/ppermute | solution.py:25
  64.0 3.7 collective-permute-start.8
  74.0 14.7 %collective-permute-start.9 = (bf16[2,512,768]{2,1,0:T(8,128)(2,1)S(1)}, bf16[2,512,768]{2,1,0:T(8,128)(2,1)S(1)}, u32[]{:S(2)}, u32[]{:S(2)}) collective-permute-start(bf16[2,512,768]{2,1,0:T(8,128)(2,1)S(1)} %get-tuple-element.110.own_ref), channel_id=1, source_target_pairs={{0,4},{4,0},{8,12},{12,8},{16,20},{20,16},{24,28},{28,24},{1,5},{5... | collective-permute-start | bytes 4718600 | tf_op jit(solution)/shard_map/ppermute | solution.py:25
  75.4 11.9 %collective-permute-start.10 = (bf16[3,96,768]{2,1,0:T(8,128)(2,1)S(1)}, bf16[3,96,768]{2,1,0:T(8,128)(2,1)S(1)}, u32[]{:S(2)}, u32[]{:S(2)}) collective-permute-start(bf16[3,96,768]{2,1,0:T(8,128)(2,1)S(1)} %get-tuple-element.227), channel_id=1, source_target_pairs={{0,8},{4,12},{8,0},{12,4},{16,24},{20,28},{24,16},{28,20},{1,9},{5... | collective-permute-start | bytes 1327112 | tf_op jit(solution)/shard_map/ppermute | solution.py:25
  77.1 11.6 %collective-permute-start.11 = (bf16[3,96,768]{2,1,0:T(8,128)(2,1)S(1)}, bf16[3,96,768]{2,1,0:T(8,128)(2,1)S(1)}, u32[]{:S(2)}, u32[]{:S(2)}) collective-permute-start(bf16[3,96,768]{2,1,0:T(8,128)(2,1)S(1)} %get-tuple-element.226), channel_id=1, source_target_pairs={{0,16},{4,20},{8,24},{12,28},{16,0},{20,4},{24,8},{28,12},{1,17},{... | collective-permute-start | bytes 1327112 | tf_op jit(solution)/shard_map/ppermute | solution.py:25
  88.8 64.4 %collective-permute-start.13 = (bf16[2,3,96,768]{3,2,1,0:T(8,128)(2,1)S(1)}, bf16[2,3,96,768]{3,2,1,0:T(8,128)(2,1)}, u32[]{:S(2)}, u32[]{:S(2)}) collective-permute-start(bf16[2,3,96,768]{3,2,1,0:T(8,128)(2,1)S(1)} %pad_maximum_fusion.4.up0.refs_7_), channel_id=1, source_target_pairs={{0,16},{4,20},{8,24},{12,28},{16,0},{20,4},{24,8},{28,12},{1,17},{... | collective-permute-start | bytes 2654216 | tf_op jit(solution)/shard_map/ppermute | solution.py:25
  91.3 61.9 %collective-permute-start.14 = (bf16[2,3,96,768]{3,2,1,0:T(8,128)(2,1)}, bf16[2,3,96,768]{3,2,1,0:T(8,128)(2,1)}, u32[]{:S(2)}, u32[]{:S(2)}) collective-permute-start(bf16[2,3,96,768]{3,2,1,0:T(8,128)(2,1)} %pad_maximum_fusion.5.down0.refs_9_), channel_id=1, source_target_pairs={{0,8},{4,12},{8,0},{12,4},{16,24},{20,28},{24,16},{28,20},{1,9},{5... | collective-permute-start | bytes 2654216 | tf_op jit(solution)/shard_map/ppermute | solution.py:25
  91.9 1.8 collective-permute-start.12
  92.0 10.3 %copy-start.20 = (bf16[256,768]{1,0:T(8,128)(2,1)S(1)}, bf16[256,768]{1,0:T(8,128)(2,1)}, u32[]{:S(2)}) copy-start(bf16[256,768]{1,0:T(8,128)(2,1)} %copy-done.19) | copy-start | bytes 1179652
  94.8 58.3 %collective-permute-start.15 = (bf16[256,768]{1,0:T(8,128)(2,1)}, bf16[256,768]{1,0:T(8,128)(2,1)}, u32[]{:S(2)}, u32[]{:S(2)}) collective-permute-start(bf16[256,768]{1,0:T(8,128)(2,1)} %get-tuple-element.119), channel_id=1, source_target_pairs={{0,0},{1,1},{2,4},{3,5},{4,2},{5,3},{6,6},{7,7},{8,8},{9,9},{10,12... | collective-permute-start | bytes 1179656 | tf_op jit(solution)/shard_map/ppermute | solution.py:46
  99.3 53.9 %collective-permute-start.16 = (bf16[256,768]{1,0:T(8,128)(2,1)}, bf16[256,768]{1,0:T(8,128)(2,1)}, u32[]{:S(2)}, u32[]{:S(2)}) collective-permute-start(bf16[256,768]{1,0:T(8,128)(2,1)} %get-tuple-element.120), channel_id=1, source_target_pairs={{0,1},{1,0},{2,5},{3,4},{4,3},{5,2},{6,7},{7,6},{8,9},{9,8},{10,13... | collective-permute-start | bytes 1179656 | tf_op jit(solution)/shard_map/ppermute | solution.py:46
  100.3 0.9 collective-permute-start.17
  101.3 34.5 %collective-permute-start.18 = (s32[256]{0:T(256)S(1)}, s32[256]{0:T(256)S(1)}, u32[]{:S(2)}, u32[]{:S(2)}) collective-permute-start(s32[256]{0:T(256)S(1)} %bitcast.176), channel_id=1, source_target_pairs={{0,1},{1,0},{2,5},{3,4},{4,3},{5,2},{6,7},{7,6},{8,9},{9,8},{10,13... | collective-permute-start | bytes 3080 | tf_op jit(solution)/shard_map/ppermute | solution.py:46
  135.8 68.8 %copy-start.8 = (bf16[512,768]{1,0:T(8,128)(2,1)}, bf16[512,768]{1,0:T(8,128)(2,1)S(1)}, u32[]{:S(2)}) copy-start(bf16[512,768]{1,0:T(8,128)(2,1)S(1)} %get-tuple-element.144.ctx_ref.refs_4_) | copy-start | bytes 2359300
  135.8 20.4 %collective-permute-start.19 = (bf16[2,3,96,768]{3,2,1,0:T(8,128)(2,1)S(1)}, bf16[2,3,96,768]{3,2,1,0:T(8,128)(2,1)}, u32[]{:S(2)}, u32[]{:S(2)}) collective-permute-start(bf16[2,3,96,768]{3,2,1,0:T(8,128)(2,1)S(1)} %pad_maximum_fusion.4.up0.refs_7_), channel_id=1, source_target_pairs={{0,4},{4,0},{8,12},{12,8},{16,20},{20,16},{24,28},{28,24},{1,5},{5... | collective-permute-start | bytes 2654216 | tf_op jit(solution)/shard_map/ppermute | solution.py:25
  153.2 3.7 collective-permute-start.21
  153.2 4.8 %collective-permute-start.20 = (bf16[2,3,96,768]{3,2,1,0:T(8,128)(2,1)}, bf16[2,3,96,768]{3,2,1,0:T(8,128)(2,1)}, u32[]{:S(2)}, u32[]{:S(2)}) collective-permute-start(bf16[2,3,96,768]{3,2,1,0:T(8,128)(2,1)} %collective-permute-done.13.up1.refs_8_), channel_id=1, source_target_pairs={{0,4},{4,0},{8,12},{12,8},{16,20},{20,16},{24,28},{28,24},{1,5},{5... | collective-permute-start | bytes 2654216 | tf_op jit(solution)/shard_map/ppermute | solution.py:25
  153.7 5.6 %collective-permute-start.22 = (bf16[2,3,96,768]{3,2,1,0:T(8,128)(2,1)}, bf16[2,3,96,768]{3,2,1,0:T(8,128)(2,1)}, u32[]{:S(2)}, u32[]{:S(2)}) collective-permute-start(bf16[2,3,96,768]{3,2,1,0:T(8,128)(2,1)} %collective-permute-done.14.down1.refs_10_), channel_id=1, source_target_pairs={{0,4},{4,0},{8,12},{12,8},{16,20},{20,16},{24,28},{28,24},{1,5},{5... | collective-permute-start | bytes 2654216 | tf_op jit(solution)/shard_map/ppermute | solution.py:25
  159.3 14.3 %copy-start.26 = (bf16[768,768]{1,0:T(8,128)(2,1)S(1)}, bf16[768,768]{1,0:T(8,128)(2,1)}, u32[]{:S(2)}) copy-start(bf16[768,768]{1,0:T(8,128)(2,1)} %param.31) | copy-start | bytes 3538948
  183.5 16.1 %collective-permute-start.25 = (bf16[2,2,4,96,768]{4,3,2,1,0:T(8,128)(2,1)}, bf16[2,2,4,96,768]{4,3,2,1,0:T(8,128)(2,1)}, u32[]{:S(2)}, u32[]{:S(2)}) collective-permute-start(bf16[2,2,4,96,768]{4,3,2,1,0:T(8,128)(2,1)} %get-tuple-element.136), channel_id=1, source_target_pairs={{0,4},{4,0},{8,12},{12,8},{16,20},{20,16},{24,28},{28,24},{1,5},{5... | collective-permute-start | bytes 7077896 | tf_op jit(solution)/shard_map/ppermute | solution.py:25
  184.0 15.7 %collective-permute-start.26 = (bf16[2,2,4,96,768]{4,3,2,1,0:T(8,128)(2,1)}, bf16[2,2,4,96,768]{4,3,2,1,0:T(8,128)(2,1)S(1)}, u32[]{:S(2)}, u32[]{:S(2)}) collective-permute-start(bf16[2,2,4,96,768]{4,3,2,1,0:T(8,128)(2,1)} %get-tuple-element.137), channel_id=1, source_target_pairs={{0,4},{4,0},{8,12},{12,8},{16,20},{20,16},{24,28},{28,24},{1,5},{5... | collective-permute-start | bytes 7077896 | tf_op jit(solution)/shard_map/ppermute | solution.py:25
  184.2 11.3 %collective-permute-start.23 = (bf16[256,768]{1,0:T(8,128)(2,1)S(1)}, bf16[256,768]{1,0:T(8,128)(2,1)S(1)}, u32[]{:S(2)}, u32[]{:S(2)}) collective-permute-start(bf16[256,768]{1,0:T(8,128)(2,1)S(1)} %get-tuple-element.229), channel_id=1, source_target_pairs={{0,0},{1,1},{4,2},{5,3},{2,4},{3,5},{6,6},{7,7},{8,8},{9,9},{12,10... | collective-permute-start | bytes 1179656 | tf_op jit(solution)/shard_map/ppermute | solution.py:51
  185.1 10.4 %collective-permute-start.24 = (bf16[256,768]{1,0:T(8,128)(2,1)S(1)}, bf16[256,768]{1,0:T(8,128)(2,1)S(1)}, u32[]{:S(2)}, u32[]{:S(2)}) collective-permute-start(bf16[256,768]{1,0:T(8,128)(2,1)S(1)} %get-tuple-element.228), channel_id=1, source_target_pairs={{1,0},{0,1},{5,2},{4,3},{3,4},{2,5},{7,6},{6,7},{9,8},{8,9},{13,10... | collective-permute-start | bytes 1179656 | tf_op jit(solution)/shard_map/ppermute | solution.py:51
  185.2 11.2 %copy-start.14 = (f32[512,768]{1,0:T(8,128)S(1)}, f32[512,768]{1,0:T(8,128)}, u32[]{:S(2)}) copy-start(f32[512,768]{1,0:T(8,128)} %copy-done.13) | copy-start | bytes 4718596
  199.6 35.0 %copy-start.11 = (bf16[512,768]{1,0:T(8,128)(2,1)}, bf16[512,768]{1,0:T(8,128)(2,1)S(1)}, u32[]{:S(2)}) copy-start(bf16[512,768]{1,0:T(8,128)(2,1)S(1)} %get-tuple-element.154.refs_6_) | copy-start | bytes 2359300
  202.1 22.6 %collective-permute-start.27 = (bf16[2,4,96,768]{3,2,1,0:T(8,128)(2,1)S(1)}, bf16[2,4,96,768]{3,2,1,0:T(8,128)(2,1)S(1)}, u32[]{:S(2)}, u32[]{:S(2)}) collective-permute-start(bf16[2,4,96,768]{3,2,1,0:T(8,128)(2,1)S(1)} %fusion.3), channel_id=1, source_target_pairs={{0,16},{4,20},{8,24},{12,28},{16,0},{20,4},{24,8},{28,12},{1,17},{... | collective-permute-start | bytes 3538952 | tf_op jit(solution)/shard_map/ppermute | solution.py:25
  202.8 22.9 %collective-permute-start.28 = (bf16[2,4,96,768]{3,2,1,0:T(8,128)(2,1)S(1)}, bf16[2,4,96,768]{3,2,1,0:T(8,128)(2,1)S(1)}, u32[]{:S(2)}, u32[]{:S(2)}) collective-permute-start(bf16[2,4,96,768]{3,2,1,0:T(8,128)(2,1)S(1)} %fusion.4), channel_id=1, source_target_pairs={{0,8},{4,12},{8,0},{12,4},{16,24},{20,28},{24,16},{28,20},{1,9},{5... | collective-permute-start | bytes 3538952 | tf_op jit(solution)/shard_map/ppermute | solution.py:25
  204.6 30.0 %copy-start.6 = (bf16[512,768]{1,0:T(8,128)(2,1)S(1)}, bf16[512,768]{1,0:T(8,128)(2,1)}, u32[]{:S(2)}) copy-start(bf16[512,768]{1,0:T(8,128)(2,1)} %copy-done.5) | copy-start | bytes 2359300
  223.6 15.8 %copy-start.2 = (bf16[512,768]{1,0:T(8,128)(2,1)}, bf16[512,768]{1,0:T(8,128)(2,1)S(1)}, u32[]{:S(2)}) copy-start(bf16[512,768]{1,0:T(8,128)(2,1)S(1)} %get-tuple-element.150.refs_1_.dq) | copy-start | bytes 2359300
  225.8 8.9 %collective-permute-start.31 = (bf16[2,512,768]{2,1,0:T(8,128)(2,1)S(1)}, bf16[2,512,768]{2,1,0:T(8,128)(2,1)S(1)}, u32[]{:S(2)}, u32[]{:S(2)}) collective-permute-start(bf16[2,512,768]{2,1,0:T(8,128)(2,1)S(1)} %get-tuple-element.152), channel_id=1, source_target_pairs={{0,4},{4,0},{8,12},{12,8},{16,20},{20,16},{24,28},{28,24},{1,5},{5... | collective-permute-start | bytes 4718600 | tf_op jit(solution)/shard_map/ppermute | solution.py:25
  239.4 22.0 %collective-permute-start.32 = (bf16[4,4,96,768]{3,2,1,0:T(8,128)(2,1)}, bf16[4,4,96,768]{3,2,1,0:T(8,128)(2,1)}, u32[]{:S(2)}, u32[]{:S(2)}) collective-permute-start(bf16[4,4,96,768]{3,2,1,0:T(8,128)(2,1)} %weigh_other.1), channel_id=1, source_target_pairs={{0,4},{4,0},{8,12},{12,8},{16,20},{20,16},{24,28},{28,24},{1,5},{5... | collective-permute-start | bytes 7077896 | tf_op jit(solution)/shard_map/ppermute | solution.py:25
  242.6 15.7 %collective-permute-start.29 = (bf16[4,96,768]{2,1,0:T(8,128)(2,1)}, bf16[4,96,768]{2,1,0:T(8,128)(2,1)}, u32[]{:S(2)}, u32[]{:S(2)}) collective-permute-start(bf16[4,96,768]{2,1,0:T(8,128)(2,1)} %slice_bitcast_fusion.2), channel_id=1, source_target_pairs={{0,8},{4,12},{8,0},{12,4},{16,24},{20,28},{24,16},{28,20},{1,9},{5... | collective-permute-start | bytes 1769480 | tf_op jit(solution)/shard_map/ppermute | solution.py:25
  246.0 15.4 %collective-permute-start.30 = (bf16[4,96,768]{2,1,0:T(8,128)(2,1)}, bf16[4,96,768]{2,1,0:T(8,128)(2,1)}, u32[]{:S(2)}, u32[]{:S(2)}) collective-permute-start(bf16[4,96,768]{2,1,0:T(8,128)(2,1)} %slice_bitcast_fusion.1), channel_id=1, source_target_pairs={{0,16},{4,20},{8,24},{12,28},{16,0},{20,4},{24,8},{28,12},{1,17},{... | collective-permute-start | bytes 1769480 | tf_op jit(solution)/shard_map/ppermute | solution.py:25
  252.1 9.4 %copy-start.47 = (bf16[2,4,96,768]{3,2,1,0:T(8,128)(2,1)S(1)}, bf16[2,4,96,768]{3,2,1,0:T(8,128)(2,1)}, u32[]{:S(2)}) copy-start(bf16[2,4,96,768]{3,2,1,0:T(8,128)(2,1)} %copy-done.46) | copy-start | bytes 3538948
  252.1 9.4 %copy-start.49 = (bf16[2,4,96,768]{3,2,1,0:T(8,128)(2,1)S(1)}, bf16[2,4,96,768]{3,2,1,0:T(8,128)(2,1)}, u32[]{:S(2)}) copy-start(bf16[2,4,96,768]{3,2,1,0:T(8,128)(2,1)} %copy-done.48) | copy-start | bytes 3538948
  254.6 8.5 %copy-start = (bf16[4,4,96,768]{3,2,1,0:T(8,128)(2,1)}, bf16[4,4,96,768]{3,2,1,0:T(8,128)(2,1)S(1)}, u32[]{:S(2)}) copy-start(bf16[4,4,96,768]{3,2,1,0:T(8,128)(2,1)S(1)} %weigh_own.1) | copy-start | bytes 7077892
  264.0 22.4 %collective-permute-start.33 = (bf16[2,2,96,768]{3,2,0,1:T(8,128)(2,1)}, bf16[2,2,96,768]{3,2,0,1:T(8,128)(2,1)}, u32[]{:S(2)}, u32[]{:S(2)}) collective-permute-start(bf16[2,2,96,768]{3,2,0,1:T(8,128)(2,1)} %fusion.11), channel_id=1, source_target_pairs={{0,1},{1,0},{2,3},{3,2},{4,5},{5,4},{6,7},{7,6},{8,9},{9,8},{10,11... | collective-permute-start | bytes 1769480 | tf_op jit(solution)/shard_map/ppermute | solution.py:29
  282.7 32.3 %all-to-all-start.1 = ((bf16[4,4,96,768]{3,2,1,0:T(8,128)(2,1)}), bf16[4,4,96,768]{3,2,1,0:T(8,128)(2,1)S(1)}, u32[]{:S(2)}, u32[]{:S(2)}) async-start(bf16[4,4,96,768]{3,2,1,0:T(8,128)(2,1)} %add_convert_fusion), calls=%async_computation.1 | async-start | bytes 4718592 | tf_op jit(solution)/shard_map/all_to_all | solution.py:64
  288.0 3.1 collective-permute-start.37
  290.1 25.5 %collective-permute-start.36 = (bf16[2,96,768]{2,1,0:T(8,128)(2,1)}, bf16[2,96,768]{2,1,0:T(8,128)(2,1)}, u32[]{:S(2)}, u32[]{:S(2)}) collective-permute-start(bf16[2,96,768]{2,1,0:T(8,128)(2,1)} %slice_bitcast_fusion.9), channel_id=1, source_target_pairs={{0,2},{1,3},{2,0},{3,1},{4,6},{5,7},{6,4},{7,5},{8,10},{9,11},{10,... | collective-permute-start | bytes 884744 | tf_op jit(solution)/shard_map/ppermute | solution.py:29
  291.2 23.1 %collective-permute-start.38 = (f32[13,768]{1,0:T(8,128)S(1)}, f32[13,768]{1,0:T(8,128)S(1)}, u32[]{:S(2)}, u32[]{:S(2)}) collective-permute-start(f32[13,768]{1,0:T(8,128)S(1)} %fusion.24), channel_id=1, source_target_pairs={{0,8},{4,12},{8,0},{12,4},{16,24},{20,28},{24,16},{28,20},{1,9},{5... | collective-permute-start | bytes 119816 | tf_op jit(solution)/shard_map/ppermute | solution.py:25
  315.6 6.8 %collective-permute-start.39 = (bf16[2,96,768]{2,1,0:T(8,128)(2,1)S(1)}, bf16[2,96,768]{2,1,0:T(8,128)(2,1)S(1)}, u32[]{:S(2)}, u32[]{:S(2)}) collective-permute-start(bf16[2,96,768]{2,1,0:T(8,128)(2,1)S(1)} %slice.217), channel_id=1, source_target_pairs={{0,1},{1,0},{2,3},{3,2},{4,5},{5,4},{6,7},{7,6},{8,9},{9,8},{10,11... | collective-permute-start | bytes 884744 | tf_op jit(solution)/shard_map/ppermute | solution.py:29
  316.2 4.3 %collective-permute-start.40 = (f32[13,768]{1,0:T(8,128)}, f32[13,768]{1,0:T(8,128)S(1)}, u32[]{:S(2)}, u32[]{:S(2)}) collective-permute-start(f32[13,768]{1,0:T(8,128)} %add.154), channel_id=1, source_target_pairs={{0,16},{4,20},{8,24},{12,28},{16,0},{20,4},{24,8},{28,12},{1,17},{... | collective-permute-start | bytes 119816 | tf_op jit(solution)/shard_map/ppermute | solution.py:25
  322.5 7.7 %collective-permute-start.43 = (bf16[96,768]{1,0:T(8,128)(2,1)S(1)}, bf16[96,768]{1,0:T(8,128)(2,1)S(1)}, u32[]{:S(2)}, u32[]{:S(2)}) collective-permute-start(bf16[96,768]{1,0:T(8,128)(2,1)S(1)} %slice_bitcast_fusion.10), channel_id=1, source_target_pairs={{0,2},{1,3},{2,0},{3,1},{4,6},{5,7},{6,4},{7,5},{8,10},{9,11},{10,... | collective-permute-start | bytes 442376 | tf_op jit(solution)/shard_map/ppermute | solution.py:29
  331.1 10.4 %all-to-all-start.2 = ((bf16[4,96,768]{2,1,0:T(8,128)(2,1)}), bf16[4,96,768]{2,1,0:T(8,128)(2,1)S(1)}, u32[]{:S(2)}, u32[]{:S(2)}) async-start(bf16[4,96,768]{2,1,0:T(8,128)(2,1)} %broadcast_in_dim.58), calls=%async_computation.2 | async-start | bytes 1179648 | tf_op jit(solution)/shard_map/all_to_all | solution.py:60
  342.6 25.9 %all-to-all-start.3 = ((bf16[4,2,96,768]{3,2,1,0:T(8,128)(2,1)}), bf16[4,2,96,768]{3,2,1,0:T(8,128)(2,1)S(1)}, u32[]{:S(2)}, u32[]{:S(2)}) async-start(bf16[4,2,96,768]{3,2,1,0:T(8,128)(2,1)} %broadcast_in_dim.59), calls=%async_computation.3 | async-start | bytes 2359296 | tf_op jit(solution)/shard_map/all_to_all | solution.py:60
  346.3 14.7 %collective-permute-start.35 = (bf16[256,768]{1,0:T(8,128)(2,1)S(1)}, bf16[256,768]{1,0:T(8,128)(2,1)S(1)}, u32[]{:S(2)}, u32[]{:S(2)}) collective-permute-start(bf16[256,768]{1,0:T(8,128)(2,1)S(1)} %copy-done.36), channel_id=1, source_target_pairs={{1,0},{0,1},{5,2},{4,3},{3,4},{2,5},{7,6},{6,7},{9,8},{8,9},{13,10... | collective-permute-start | bytes 1179656 | tf_op jit(solution)/shard_map/ppermute | solution.py:51
  346.4 14.7 %collective-permute-start.34 = (bf16[256,768]{1,0:T(8,128)(2,1)S(1)}, bf16[256,768]{1,0:T(8,128)(2,1)}, u32[]{:S(2)}, u32[]{:S(2)}) collective-permute-start(bf16[256,768]{1,0:T(8,128)(2,1)S(1)} %copy-done.34), channel_id=1, source_target_pairs={{0,0},{1,1},{4,2},{5,3},{2,4},{3,5},{6,6},{7,7},{8,8},{9,9},{12,10... | collective-permute-start | bytes 1179656 | tf_op jit(solution)/shard_map/ppermute | solution.py:51
  347.8 11.6 %collective-permute-start.41 = (f32[13,768]{1,0:T(8,128)}, f32[13,768]{1,0:T(8,128)S(1)}, u32[]{:S(2)}, u32[]{:S(2)}) collective-permute-start(f32[13,768]{1,0:T(8,128)} %add.155), channel_id=1, source_target_pairs={{0,1},{1,0},{2,3},{3,2},{4,5},{5,4},{6,7},{7,6},{8,9},{9,8},{10,11... | collective-permute-start | bytes 119816 | tf_op jit(solution)/shard_map/ppermute | solution.py:29
  349.8 21.5 %collective-permute-start.44 = (bf16[4,96,768]{2,1,0:T(8,128)(2,1)S(1)}, bf16[4,96,768]{2,1,0:T(8,128)(2,1)S(1)}, u32[]{:S(2)}, u32[]{:S(2)}) collective-permute-start(bf16[4,96,768]{2,1,0:T(8,128)(2,1)S(1)} %all-to-all-done.2), channel_id=1, source_target_pairs={{0,4},{4,0},{8,12},{12,8},{16,20},{20,16},{24,28},{28,24},{1,5},{5... | collective-permute-start | bytes 1769480 | tf_op jit(solution)/shard_map/ppermute | solution.py:25
  360.2 7.6 %collective-permute-start.42 = (f32[13,768]{1,0:T(8,128)S(1)}, f32[13,768]{1,0:T(8,128)S(1)}, u32[]{:S(2)}, u32[]{:S(2)}) collective-permute-start(f32[13,768]{1,0:T(8,128)S(1)} %add.156), channel_id=1, source_target_pairs={{0,2},{1,3},{2,0},{3,1},{4,6},{5,7},{6,4},{7,5},{8,10},{9,11},{10,... | collective-permute-start | bytes 119816 | tf_op jit(solution)/shard_map/ppermute | solution.py:29
  368.6 5.1 %collective-permute-start.45 = (bf16[4,2,96,768]{3,2,0,1:T(8,128)(2,1)S(1)}, bf16[4,2,96,768]{3,2,0,1:T(8,128)(2,1)S(1)}, u32[]{:S(2)}, u32[]{:S(2)}) collective-permute-start(bf16[4,2,96,768]{3,2,0,1:T(8,128)(2,1)S(1)} %copy.59), channel_id=1, source_target_pairs={{0,4},{4,0},{8,12},{12,8},{16,20},{20,16},{24,28},{28,24},{1,5},{5... | collective-permute-start | bytes 3538952 | tf_op jit(solution)/shard_map/ppermute | solution.py:25
  (61 other events, 155.7 us)
